TPU v7x, 256 devices: a whole 4x4x8 slice. The times are simulated.
256 devices in a mesh: req: 8 (over y, core), tp: 32 (over z, x).
Axes of the slice: x: 4, y: 4, z: 8, core: 2. Of those that a mesh axis runs over, the one named last changes fastest.
Arguments:
- queries: bfloat16 [1024, 1536], P(('req', 'tp')), may hold values from -8 to 8
- new_kv: bfloat16 [1024, 1024], P(('req', 'tp')), may hold values from -6 to 6
- residual: bfloat16 [1024, 1536], P(('req', 'tp')), may hold values from -6 to 6
- placement: int32 [16], P('req'), may hold values from 0 to 15, as said below
- lengths: int32 [16], P('req'), may hold values from 2 to 4096
- page_table: int32 [16, 1, 32], P('req', None, 'tp'), may hold values from 0 to 1, as said below
- cache_keys: bfloat16 [512, 128, 512], P(('req', 'tp')), may hold values from -6 to 6
- cache_values: bfloat16 [512, 128, 512], P(('req', 'tp')), may hold values from -6 to 6
- parents: int32 [16, 64], P('req'), may hold values from 0 to 62, as said below
- accept_leaf: int32 [16], P('req'), may hold values from 0 to 63
- out_weight: bfloat16 [1536, 1536], replicated, may hold values from -0.15625 to 0.15625
- norm_gain: float32 [1536], replicated, may hold values from 0.1 to 1.9
- router_weight: bfloat16 [1536, 40], replicated, may hold values from -0.15625 to 0.15625
- expert_ids: int32 [1024, 8], P('req'), may hold values from 0 to 39, all different within a row
- gate_up: bfloat16 [160, 1536, 256], P('tp'), may hold values from -0.15625 to 0.15625
- down_weight: bfloat16 [160, 128, 1536], P('tp'), may hold values from -0.25 to 0.25
Outputs:
- attn_out: bfloat16 [1024, 1536], P(('req', 'tp'))
- layer_out: bfloat16 [1024, 1536], P(('req', 'tp'))
- accepted_kv: bfloat16 [1024, 1024], P(('req', 'tp'))
Inputs may be any that keep to these rules, and one draw needn't show every extreme that they name: `placement`: slot s of each group of 2 slots holds a request whose index is s modulo 2; every request is held once. `page_table`: within each group of 2 slots and each last index, the 2 entries are distinct. parents[s, n] < n for n > 0; parents[s, 0] = 0.
All inputs are finite; a program needn't handle non-finite values.
Results may differ from a plain program's by a relative error of at most 0.01.
Values may be sent and summed in bfloat16 or wider, within the bound.
A program may use at most 128 MiB of HBM per device.

v0:
```python
import math

import jax
import jax.numpy as jnp
from jax import lax
from jax.sharding import PartitionSpec as P

HEADS = 24
KV_HEADS = 8
HEAD = 64
FF_E = 512
UNIT = 128
DRAFT = 64


neg_big = -1e30
norm_eps = 1e-06


def joined_2(part, axis, combine):
    gathered = jax.tree.map(lambda a: lax.all_gather(a, axis), part)

    def take(source):
        return jax.tree.map(lambda a: lax.dynamic_index_in_dim(a, source, 0, False), gathered)

    return lax.fori_loop(
        1, lax.axis_size(axis), lambda source, state: combine(state, take(source)), take(0)
    )


def ancestry(parents):
    node_count = parents.shape[-1]
    node_ids = jnp.arange(node_count, dtype=jnp.int32)
    linked = (parents[:, :, None] == node_ids[None, None, :]) & (node_ids[None, :, None] > 0)
    reached = jnp.maximum(linked.astype(jnp.float32), jnp.eye(node_count, dtype=jnp.float32)[None])
    for _ in range(node_count.bit_length()):
        reached = jnp.minimum(
            jnp.einsum("rnm,rmk->rnk", reached, reached, precision=lax.Precision.HIGHEST), 1.0
        )
    return reached


def combine_stats(left_stats, right_stats):
    left_max, left_sum, left_out = left_stats
    right_max, right_sum, right_out = right_stats
    top_score = jnp.maximum(left_max, right_max)
    left_scale = jnp.exp(left_max - top_score)
    right_scale = jnp.exp(right_max - top_score)
    row_count, head_count = left_max.shape
    out_sum = (
        left_out.reshape(row_count, head_count, -1) * left_scale[..., None]
        + right_out.reshape(row_count, head_count, -1) * right_scale[..., None]
    )
    return (
        top_score,
        left_sum * left_scale + right_sum * right_scale,
        out_sum.reshape(row_count, -1),
    )


def finish_rows(stat_sum, stat_out):
    row_count, head_count = stat_sum.shape
    return (
        (stat_out.reshape(row_count, head_count, -1) / stat_sum[..., None])
        .reshape(row_count, -1)
        .astype(jnp.bfloat16)
    )


def project_rows(attn_rows, res_rows, out_weight):
    return res_rows.astype(jnp.float32) + jnp.dot(
        attn_rows, out_weight, preferred_element_type=jnp.float32
    )


def rms_normed(hidden, norm_gain):
    scale_rows = lax.rsqrt(jnp.mean(hidden * hidden, axis=-1, keepdims=True) + norm_eps)
    return (hidden * scale_rows * norm_gain).astype(jnp.bfloat16)


def unit_shares(normed_all, router_weight, expert_ids, tp_rank, units_dev):
    logits = jnp.dot(normed_all, router_weight, preferred_element_type=jnp.float32)
    expert_range = jnp.arange(router_weight.shape[1], dtype=jnp.int32)
    onehot = (expert_ids[:, :, None] == expert_range[None, None, :]).astype(jnp.float32)
    chosen = jnp.sum(logits[:, None, :] * onehot, axis=-1)
    expo_chosen = jnp.exp(chosen)
    expert_probs = expo_chosen / jnp.sum(expo_chosen, axis=-1, keepdims=True)
    routing = jnp.sum(expert_probs[:, :, None] * onehot, axis=1)
    unit_ids = tp_rank * units_dev + jnp.arange(units_dev, dtype=jnp.int32)
    expert_of_unit = unit_ids // (FF_E // UNIT)
    pick = (expert_range[:, None] == expert_of_unit[None, :]).astype(jnp.float32)
    return jnp.dot(routing, pick, precision=lax.Precision.HIGHEST)


def per_device(
    queries,
    new_kv,
    residual,
    placement,
    lengths,
    page_table,
    cache_keys,
    cache_values,
    parents,
    accept_leaf,
    out_weight,
    norm_gain,
    router_weight,
    expert_ids,
    gate_up,
    down_weight,
):
    tok_dev = queries.shape[0]
    tp_count = lax.axis_size("tp")
    tp_rank = lax.axis_index("tp")
    group_rows = tok_dev * tp_count
    slot_count = placement.shape[0]
    kv_width = cache_keys.shape[2]
    page_len = cache_keys.shape[1]
    group_size = HEADS // KV_HEADS
    score_scale = 1.0 / math.sqrt(HEAD)
    row_start = tp_rank * tok_dev
    pulled_q, pulled_kv, pulled_res = (
        lax.all_gather(queries, "req", axis=0, tiled=True),
        lax.all_gather(new_kv, "req", axis=0, tiled=True),
        lax.all_gather(residual, "req", axis=0, tiled=True),
    )
    row_offsets = jnp.arange(tok_dev, dtype=jnp.int32)
    row_pos = row_start + row_offsets
    row_slot = row_pos // DRAFT
    slot_match = row_slot[:, None] == jnp.arange(slot_count, dtype=jnp.int32)[None, :]
    source_group = jnp.sum(jnp.where(slot_match, placement[None, :] // slot_count, 0), axis=1)
    source_rows = source_group * tok_dev + row_offsets
    own_q = jnp.take(pulled_q, source_rows, axis=0)
    own_kv = jnp.take(pulled_kv, source_rows, axis=0)
    own_res = jnp.take(pulled_res, source_rows, axis=0)
    all_q, all_kv = (
        lax.all_gather(own_q, "tp", axis=0, tiled=True),
        lax.all_gather(own_kv, "tp", axis=0, tiled=True),
    )
    local_pages = page_table.shape[1]
    page_ids = page_table[:, :, 0].reshape(-1)
    keys_local = jnp.take(cache_keys, page_ids, axis=0).reshape(
        slot_count, local_pages, page_len, KV_HEADS, HEAD
    )
    values_local = jnp.take(cache_values, page_ids, axis=0).reshape(
        slot_count, local_pages, page_len, KV_HEADS, HEAD
    )
    query_blocks = all_q.reshape(slot_count, DRAFT, KV_HEADS, group_size, HEAD)
    scores = (
        jnp.einsum(
            "sqgrd,sltgd->sqgrlt", query_blocks, keys_local, preferred_element_type=jnp.float32
        )
        * score_scale
    )
    positions = (
        jnp.arange(local_pages, dtype=jnp.int32)[:, None] * tp_count + tp_rank
    ) * page_len + jnp.arange(page_len, dtype=jnp.int32)[None, :]
    is_valid = (positions[None] < lengths[:, None, None])[:, None, None, None]
    scores = jnp.where(is_valid, scores, neg_big)
    block_max = jnp.max(scores, axis=-1)
    weights = jnp.where(is_valid, jnp.exp(scores - block_max[..., None]), 0.0).astype(jnp.bfloat16)
    block_sum = jnp.sum(weights.astype(jnp.float32), axis=-1)
    block_out = jnp.einsum(
        "sqgrlt,sltgd->sqgrld", weights, values_local, preferred_element_type=jnp.float32
    )
    page_top = jnp.max(block_max, axis=-1)
    page_scale = jnp.exp(block_max - page_top[..., None])
    stat_max = page_top.reshape(group_rows, HEADS)
    stat_sum = jnp.sum(block_sum * page_scale, axis=-1).reshape(group_rows, HEADS)
    stat_out = jnp.sum(block_out * page_scale[..., None], axis=-2).reshape(group_rows, HEADS * HEAD)
    reached = ancestry(parents)
    reach_rows = jnp.take(reached.reshape(slot_count * DRAFT, DRAFT), row_pos, axis=0)
    key_slot = jnp.arange(group_rows, dtype=jnp.int32) // DRAFT
    same_slot = key_slot[None, :] == row_slot[:, None]
    allowed = same_slot & (jnp.tile(reach_rows, (1, slot_count)) > 0.5)
    tree_keys = all_kv[:, :kv_width].reshape(group_rows, KV_HEADS, HEAD)
    tree_values = all_kv[:, kv_width:].reshape(group_rows, KV_HEADS, HEAD)
    own_blocks = own_q.reshape(tok_dev, KV_HEADS, group_size, HEAD)
    tree_scores = (
        jnp.einsum("igrd,kgd->igrk", own_blocks, tree_keys, preferred_element_type=jnp.float32)
        * score_scale
    )
    tree_mask = allowed[:, None, None, :]
    tree_scores = jnp.where(tree_mask, tree_scores, neg_big)
    tree_max = jnp.max(tree_scores, axis=-1)
    tree_weights = jnp.where(tree_mask, jnp.exp(tree_scores - tree_max[..., None]), 0.0).astype(
        jnp.bfloat16
    )
    tree_sum = jnp.sum(tree_weights.astype(jnp.float32), axis=-1)
    tree_out = jnp.einsum(
        "igrk,kgd->igrd", tree_weights, tree_values, preferred_element_type=jnp.float32
    )
    own_stats = (
        lax.dynamic_slice_in_dim(stat_max, row_start, tok_dev, 0),
        lax.dynamic_slice_in_dim(stat_sum, row_start, tok_dev, 0),
        lax.dynamic_slice_in_dim(stat_out, row_start, tok_dev, 0),
    )
    tree_stats = (
        tree_max.reshape(tok_dev, HEADS),
        tree_sum.reshape(tok_dev, HEADS),
        tree_out.reshape(tok_dev, HEADS * HEAD),
    )
    joined = combine_stats(own_stats, tree_stats)
    stat_max = lax.dynamic_update_slice_in_dim(stat_max, joined[0], row_start, 0)
    stat_sum = lax.dynamic_update_slice_in_dim(stat_sum, joined[1], row_start, 0)
    stat_out = lax.dynamic_update_slice_in_dim(stat_out, joined[2], row_start, 0)
    normed_all = None
    merged = joined_2((stat_max, stat_sum, stat_out), "tp", combine_stats)
    attn_own = finish_rows(
        lax.dynamic_slice_in_dim(merged[1], row_start, tok_dev, 0),
        lax.dynamic_slice_in_dim(merged[2], row_start, tok_dev, 0),
    )
    hidden_own = project_rows(attn_own, own_res, out_weight)
    normed_own = rms_normed(hidden_own, norm_gain)
    units_dev = gate_up.shape[0]
    unit_width = gate_up.shape[2] // 2
    normed_all = lax.all_gather(normed_own, "tp", axis=0, tiled=True)
    shares = unit_shares(normed_all, router_weight, expert_ids, tp_rank, units_dev)
    gate_both = jnp.einsum("td,udh->tuh", normed_all, gate_up, preferred_element_type=jnp.float32)
    activated = (
        jax.nn.silu(gate_both[..., :unit_width]) * gate_both[..., unit_width:] * shares[:, :, None]
    ).astype(jnp.bfloat16)
    moe_own = lax.psum_scatter(
        jnp.einsum("tuh,uhd->td", activated, down_weight, preferred_element_type=jnp.float32),
        "tp",
        scatter_dimension=0,
        tiled=True,
    )
    layer_out = (hidden_own + moe_own).astype(jnp.bfloat16)
    node_ids = jnp.arange(DRAFT, dtype=jnp.int32)
    leaf_pick = (accept_leaf[:, None] == node_ids[None, :]).astype(jnp.float32)
    path_weight = jnp.einsum("sn,snk->sk", leaf_pick, reached, precision=lax.Precision.HIGHEST)
    path_flags = (path_weight > 0.5).astype(jnp.int32)
    path_rank = jnp.cumsum(path_flags, axis=1) - 1
    chosen_node = (path_flags[:, None, :] > 0) & (path_rank[:, None, :] == node_ids[None, :, None])
    own_choice = jnp.take(chosen_node.reshape(slot_count * DRAFT, DRAFT), row_pos, axis=0)
    spread = same_slot & jnp.tile(own_choice, (1, slot_count))
    accepted = jnp.dot(
        spread.astype(jnp.bfloat16), all_kv, preferred_element_type=jnp.float32
    ).astype(jnp.bfloat16)
    return (attn_own, layer_out, accepted)


def solution(mesh):
    in_specs = (
        P(("req", "tp"), None),
        P(("req", "tp"), None),
        P(("req", "tp"), None),
        P("req"),
        P("req"),
        P("req", None, "tp"),
        P(("req", "tp"), None, None),
        P(("req", "tp"), None, None),
        P("req", None),
        P("req"),
        P(),
        P(),
        P(),
        P("req", None),
        P("tp", None, None),
        P("tp", None, None),
    )
    out_specs = (P(("req", "tp"), None), P(("req", "tp"), None), P(("req", "tp"), None))
    return jax.shard_map(
        per_device, mesh=mesh, in_specs=in_specs, out_specs=out_specs, check_vma=False
    )
```

profile of v0, /device:TPU:2, one launch (start us, length us, event | category | flops | bytes accessed | tf_op | source)
XLA Modules:
  0.0 734.6 jit_solution(6289044526441213164)
XLA Ops:
  12.0 13.5 %all-gather = bf16[8,4,1536]{2,1,0:T(4,128)(2,1)S(1)} all-gather(bf16[1,4,1536]{2,1,0:T(4,128)(2,1)} %bitcast.182), channel_id=1, replica_groups=mesh['req'=8,'tp'=32] {'req'}, dimensions={0}, use_global_device_ids=true | all-gather | bytes 110592 | tf_op jit(solution)/shard_map/all_gather | solution.py:124
  26.3 1.5 gather_fusion.5
  27.8 1.5 gather_fusion.3
  31.0 52.2 %all-gather.1 = bf16[32,4,1536]{2,1,0:T(4,128)(2,1)S(1)} all-gather(bf16[1,4,1536]{2,1,0:T(4,128)(2,1)S(1)} %fusion.72), channel_id=1, replica_groups=mesh['req'=8,'tp'=32] {'tp'}, dimensions={0}, use_global_device_ids=true | all-gather | bytes 405504 | tf_op jit(solution)/shard_map/all_gather | solution.py:138
  83.2 1.6 reshape.450
  84.9 2.0 bitcast_reduce_fusion
  88.1 1.8 copy.183
  89.9 2.4 convert_reduce_fusion
  94.6 1.8 reshape.459
  96.4 1.8 all_gather.49
  105.6 12.9 %all-gather.2 = bf16[8,4,1024]{2,1,0:T(4,128)(2,1)S(1)} all-gather(bf16[1,4,1024]{2,1,0:T(4,128)(2,1)} %bitcast.184), channel_id=1, replica_groups=mesh['req'=8,'tp'=32] {'req'}, dimensions={0}, use_global_device_ids=true | all-gather | bytes 73728 | tf_op jit(solution)/shard_map/all_gather | solution.py:125
  119.4 47.1 %all-gather.3 = bf16[32,4,1024]{2,1,0:T(4,128)(2,1)S(1)} all-gather(bf16[1,4,1024]{2,1,0:T(4,128)(2,1)S(1)} %select_bitcast_fusion), channel_id=1, replica_groups=mesh['req'=8,'tp'=32] {'tp'}, dimensions={0}, use_global_device_ids=true | all-gather | bytes 270336 | tf_op jit(solution)/shard_map/all_gather | solution.py:139
  170.9 1.6 fusion.8
  172.6 4.6 dynamic_update_slice.14
  178.9 12.7 %all-gather.4 = bf16[8,4,1536]{2,1,0:T(4,128)(2,1)S(1)} all-gather(bf16[1,4,1536]{2,1,0:T(4,128)(2,1)S(1)} %bitcast.183), channel_id=1, replica_groups=mesh['req'=8,'tp'=32] {'req'}, dimensions={0}, use_global_device_ids=true | all-gather | bytes 110592 | tf_op jit(solution)/shard_map/all_gather | solution.py:126
  193.8 52.6 %all_gather.46 = f32[32,128,24]{1,2,0:T(8,128)} all-gather(f32[1,128,24]{1,2,0:T(8,128)S(1)} %dynamic_update_slice.12), channel_id=1, replica_groups=mesh['req'=8,'tp'=32] {'tp'}, dimensions={0}, use_global_device_ids=true | all-gather | bytes 405504 | tf_op jit(solution)/shard_map/all_gather | solution.py:21
  246.4 52.0 %all_gather.48 = f32[32,128,24]{1,2,0:T(8,128)} all-gather(f32[1,128,24]{1,2,0:T(8,128)S(1)} %dynamic_update_slice.13), channel_id=1, replica_groups=mesh['req'=8,'tp'=32] {'tp'}, dimensions={0}, use_global_device_ids=true | all-gather | bytes 405504 | tf_op jit(solution)/shard_map/all_gather | solution.py:21
  301.1 61.4 %all-gather.8.cloned.1.call-done = f32[32,128,1536]{2,1,0:T(8,128)} async-done(((f32[1,128,1536]{2,1,0:T(8,128)}), f32[32,128,1536]{2,1,0:T(8,128)}) %all-gather.8.cloned.1.call-update) | async-done | bytes 25165840 | tf_op jit(solution)/shard_map/all_gather | solution.py:21
  364.9 156.1 %while.19 = (s32[]{:T(128)}, f32[128,24]{0,1:T(8,128)}, f32[128,24]{0,1:T(8,128)}, f32[128,1536]{0,1:T(8,128)}, f32[32,128,24]{1,2,0:T(8,128)}, /*index=5*/f32[3...) while((s32[]{:T(128)}, f32[128,24]{0,1:T(8,128)}, f32[128,24]{0,1:T(8,128)}, ...), condition=%wide.region_6.9_spmd, body=%wide.region_5.8_spmd.sunk | while | flops 608261 | bytes 5628047 | solution.py:26
  367.7 2.2 fusion.76
  372.8 2.2 fusion.76
  375.0 1.4 fusion.75
  377.8 2.2 fusion.76
  382.8 2.2 fusion.76
  387.9 2.2 fusion.76
  392.9 2.2 fusion.76
  395.1 1.4 fusion.75
  398.0 2.2 fusion.76
  400.2 1.4 fusion.75
  403.0 2.2 fusion.76
  408.0 2.2 fusion.76
  413.1 2.2 fusion.76
  415.3 1.4 fusion.75
  418.1 2.2 fusion.76
  423.1 2.2 fusion.76
  428.2 2.2 fusion.76
  433.2 2.2 fusion.76
  435.4 1.4 fusion.75
  438.2 2.2 fusion.76
  440.5 1.4 fusion.75
  443.3 2.2 fusion.76
  448.3 2.2 fusion.76
  453.4 2.2 fusion.76
  458.4 2.2 fusion.76
  463.4 2.2 fusion.76
  468.5 2.2 fusion.76
  473.5 2.2 fusion.76
  478.5 2.2 fusion.76
  480.7 1.4 fusion.75
  483.6 2.2 fusion.76
  488.6 2.2 fusion.76
  493.7 2.2 fusion.76
  498.7 2.2 fusion.76
  503.7 2.2 fusion.76
  508.8 2.2 fusion.76
  513.8 2.2 fusion.76
  518.8 2.2 fusion.76
  522.1 1.4 copy.194
  523.6 3.2 multiply_reduce_fusion
  526.9 48.1 %all-gather.5 = bf16[32,4,1536]{2,1,0:T(4,128)(2,1)S(1)} all-gather(bf16[1,4,1536]{2,1,0:T(4,128)(2,1)S(1)} %fusion.30), channel_id=1, replica_groups=mesh['req'=8,'tp'=32] {'tp'}, dimensions={0}, use_global_device_ids=true | all-gather | bytes 405504 | tf_op jit(solution)/shard_map/all_gather | solution.py:218
  575.7 2.8 fusion.44
  578.6 1.4 convolution_bitcast_fusion
  582.3 144.0 %all-reduce.3.cloned.1.call-done = f32[128,1536]{1,0:T(8,128)} async-done(((f32[128,1536]{1,0:T(8,128)}), f32[128,1536]{1,0:T(8,128)}) %all-reduce.3.cloned.1.call-update) | async-done | bytes 786448
  726.3 1.4 fusion.26
  (264 shorter events, 113.2 us)
Async XLA Ops:
  7.2 571.4 %copy-start = (bf16[5,128,1536]{2,1,0:T(8,128)(2,1)S(1)}, bf16[5,128,1536]{2,1,0:T(8,128)(2,1)}, u32[]{:S(2)}) copy-start(bf16[5,128,1536]{2,1,0:T(8,128)(2,1)} %param.37) | copy-start | bytes 5898244
  7.2 355.3 %all-gather.8.cloned.1.call-start = ((), (), s32[]{:S(2)}) async-start(), calls=%async_computation | async-start | bytes 25952256 | tf_op jit(solution)/shard_map/all_gather | solution.py:21
  7.2 3.6 copy-start.26
  11.4 107.8 %copy-start.20 = (pred[4]{0:T(512)(128)(4,1)}, pred[4]{0:T(512)(128)(4,1)S(1)}, u32[]{:S(2)}) copy-start(pred[4]{0:T(512)(128)(4,1)S(1)} %get-tuple-element.230) | copy-start | bytes 16
  12.0 14.2 %copy-start.22 = (s32[1024]{0:T(1024)}, s32[1024]{0:T(1024)S(1)}, u32[]{:S(2)}) copy-start(s32[1024]{0:T(1024)S(1)} %pad_clamp_fusion.2) | copy-start | bytes 12292
  29.3 55.5 %copy-start.31 = (s32[2]{0:T(128)S(1)}, s32[2]{0:T(128)}, u32[]{:S(2)}) copy-start(s32[2]{0:T(128)} %param.26) | copy-start | bytes 28
  84.9 3.2 copy-start.23
  86.9 0.6 copy-start.5
  89.9 2.4 copy-start.2
  89.9 2.4 copy-start.6
  89.9 2.4 copy-start.11
  89.9 2.4 copy-start.24
  101.9 65.0 %copy-start.27 = (s32[4]{0:T(128)S(1)}, s32[4]{0:T(128)}, u32[]{:S(2)}) copy-start(s32[4]{0:T(128)} %copy-done.26) | copy-start | bytes 52
  101.9 65.0 %copy-start.29 = (s32[128]{0:T(128)S(1)}, s32[128]{0:T(128)}, u32[]{:S(2)}) copy-start(s32[128]{0:T(128)} %and_select_fusion.1) | copy-start | bytes 1540
  103.7 64.1 %copy-start.7 = (f32[2,64,8,3]{1,0,3,2:T(2,128)S(1)}, f32[2,64,8,3]{1,0,3,2:T(2,128)}, u32[]{:S(2)}) copy-start(f32[2,64,8,3]{1,0,3,2:T(2,128)} %copy.169) | copy-start | bytes 36868
  118.6 49.5 %copy-start.12 = (f32[2,64,8,3]{1,3,2,0:T(4,128)S(1)}, f32[2,64,8,3]{1,3,2,0:T(4,128)}, u32[]{:S(2)}) copy-start(f32[2,64,8,3]{1,3,2,0:T(4,128)} %convert_reduce_fusion) | copy-start | bytes 36868
  166.5 2.5 copy-start.3
  168.1 0.9 copy-start.9
  169.7 2.9 copy-start.1
  177.2 1.5 copy-start.8
  177.2 1.6 copy-start.10
  177.2 1.7 copy-start.17
  177.2 15.7 %copy-start.19 = (f32[1,4,24]{2,1,0:T(4,128)S(1)}, f32[1,4,24]{2,1,0:T(4,128)}, u32[]{:S(2)}) copy-start(f32[1,4,24]{2,1,0:T(4,128)} %get-tuple-element.236) | copy-start | bytes 1156
  178.5 547.8 %all-reduce.3.cloned.1.call-start = ((), (), s32[]{:S(2)}) async-start(), calls=%async_computation.1 | async-start | bytes 1572864
  521.0 2.5 copy-start.14
  521.0 2.5 copy-start.21
  523.5 3.2 copy-start.15
  523.6 3.2 copy-start.18
  526.8 48.4 %copy-start.13 = (bf16[1536,40]{0,1:T(8,128)(2,1)S(1)}, bf16[1536,40]{0,1:T(8,128)(2,1)}, u32[]{:S(2)}) copy-start(bf16[1536,40]{0,1:T(8,128)(2,1)} %param.34) | copy-start | bytes 368644
  526.8 48.6 %copy-start.16 = (s32[128,8]{0,1:T(8,128)S(1)}, s32[128,8]{0,1:T(8,128)}, u32[]{:S(2)}) copy-start(s32[128,8]{0,1:T(8,128)} %param.35) | copy-start | bytes 12292
  578.6 1.5 copy-start.25
  578.6 1.6 copy-start.32
  578.6 2.8 copy-start.4
  578.6 2.8 copy-start.28
  578.6 2.8 copy-start.30
Sparse Core Ops, SparseCore 0:
  178.6 183.8 all-gather.7
  580.2 146.0 all-reduce.2
where the time goes:
time: 741 us; the launch traced here: 735 us
  blocking collectives  291 us (39%)
  waiting for transfers between devices  205 us (28%)
  other arithmetic  128 us (17%)
  local copies, waits for them, and re-layouts  79.6 us (11%)
  between operations  15.4 us (2%)
  matrix products  14.5 us (2%)
    unnamed x3, waiting for transfers between devices  144 us
    all_gather x2, blocking collectives, joined_2(): gathered = jax.tree.map(lambda a: lax.all_gather(a, axis), part)  105 us
    add x32, other arithmetic, combine_stats(): left_out.reshape(row_count, head_count, -1) * left_scale[..., None]  70.1 us
    all_gather x1, waiting for transfers between devices, joined_2(): gathered = jax.tree.map(lambda a: lax.all_gather(a, axis), part)  61.4 us
    all_gather x1, blocking collectives, per_device(): lax.all_gather(own_q, 'tp', axis=0, tiled=True)  52.2 us
    all_gather x1, blocking collectives, per_device(): normed_all = lax.all_gather(normed_own, 'tp', axis=0, tiled=True)  48.1 us
    all_gather x1, blocking collectives, per_device(): lax.all_gather(own_kv, 'tp', axis=0, tiled=True)  47.1 us
    dynamic_slice x62, local copies, waits for them, and re-layouts, take(): lax.dynamic_index_in_dim(a, source, 0, False)  44.7 us
  transfers between devices with their start and end apart: 2, of which 2 were waited for; matrix products, arithmetic and copies ran while one was open for 1% of the time, Pallas kernels for 0%

commit v1 on v0

v1 whole, which is shorter than its diff:
```python
import jax
import jax.numpy as jnp
from jax import lax
from jax.experimental import pallas as pl
from jax.experimental.pallas import tpu as pltpu
from jax.sharding import PartitionSpec as P

HEADS = 24
KV_HEADS = 8
HEAD = 64
D = 1536
EXPERTS = 40
FF_E = 512
UNIT = 128
UNITS_DEV = 5
DRAFT = 64
PAGE = 128
N_REQ = 8
N_TP = 32
TOK = 4
CHUNKS = 4
CW = D // CHUNKS
HALF = N_TP // 2
ROWS = CHUNKS * TOK
GROUP = N_TP * TOK

neg_big = -1e30
norm_eps = 1e-06
MESH = pl.DeviceIdType.MESH
f32 = jnp.float32
bf16 = jnp.bfloat16


def iota(shape, dim):
    return lax.broadcasted_iota(jnp.int32, shape, dim)


def ones_at(mask):
    return jnp.where(mask, 1.0, 0.0).astype(bf16)


def dot(a, b):
    return jnp.dot(a, b, preferred_element_type=f32)


def dot_t(a, b):
    return lax.dot_general(a, b, (((1,), (1,)), ((), ())), preferred_element_type=f32)


def softmax_block(stacked, keys, values, lo, hi, ones_rhs, valid):
    count = keys.shape[0]
    keys_two = jnp.concatenate([keys * lo, keys * hi], axis=0)
    values_two = jnp.concatenate([values * lo, values * hi], axis=0)
    scores = dot_t(stacked, keys_two)
    s_lo = jnp.where(valid, scores[:, :count], neg_big)
    s_hi = jnp.where(valid, scores[:, count:], neg_big)
    m_lo = jnp.max(s_lo, axis=1, keepdims=True)
    m_hi = jnp.max(s_hi, axis=1, keepdims=True)
    w_lo = jnp.where(valid, jnp.exp(s_lo - m_lo), 0.0).astype(bf16)
    w_hi = jnp.where(valid, jnp.exp(s_hi - m_hi), 0.0).astype(bf16)
    weights = jnp.concatenate([w_lo, w_hi], axis=1)
    both = dot(weights, jnp.concatenate([values_two, ones_rhs], axis=1))
    out, total = both[:, :128], both[:, 128:]
    rows = out.shape[0]
    first = iota((rows, 128), 1) < HEAD
    top = jnp.where(first, m_lo, m_hi)
    some = total > 0.0
    safe = jnp.where(some, total, 1.0)
    return out / safe, jnp.where(some, top + jnp.log(safe), neg_big)


def two_ones(count):
    row = iota((2 * count, 128), 0)
    lane = iota((2 * count, 128), 1)
    return ones_at((row >= count) == (lane >= HEAD))


def kernel(
    placement, lengths, table, leaf,
    q_ref, kv_ref, res_ref, par_ref, gain_ref, ids_ref,
    keys_hbm, vals_hbm, ow_hbm, rw_hbm, gu_hbm, dw_hbm,
    attn_ref, layer_ref, acc_ref,
    kbuf, vbuf, ow, rw, gu, dw,
    q8, r8, qall, kvall, osend, orecv, nall, msend, mrecv,
    chunk_s, flat_s, res_s, perm_s, permt_s, outs_s, nfull, act_s, moe_s,
    wsem, s_q8, r_q8, s_r8, r_r8, s_q, r_q, s_kv, r_kv, s_o, r_o, s_n, r_n, s_m, r_m,
):
    g = lax.axis_index("req")
    t = lax.axis_index("tp")
    half = t // HALF
    t_in = t % HALF

    def req_peer(k):
        return lax.rem(g + k, N_REQ)

    def tp_peer(k):
        return lax.rem(t // 4 + k // 4, 8) * 4 + lax.rem(t % 4 + k % 4, 4)

    def slot_peer(k):
        return half * HALF + lax.rem(t_in + k, HALF)

    barrier = pltpu.get_barrier_semaphore()

    def greet_req(k, carry):
        pl.semaphore_signal(barrier, inc=1, device_id={"req": req_peer(k)}, device_id_type=MESH)
        return carry

    def greet_tp(k, carry):
        pl.semaphore_signal(barrier, inc=1, device_id={"tp": tp_peer(k)}, device_id_type=MESH)
        return carry

    lax.fori_loop(1, N_REQ, greet_req, 0)
    lax.fori_loop(1, N_TP, greet_tp, 0)

    loads = [
        pltpu.make_async_copy(a, b, wsem.at[i])
        for i, (a, b) in enumerate(
            [(keys_hbm, kbuf), (vals_hbm, vbuf), (ow_hbm, ow), (rw_hbm, rw), (gu_hbm, gu), (dw_hbm, dw)]
        )
    ]
    for load in loads:
        load.start()

    q_in = q_ref[...].astype(f32) * (HEAD ** -0.5)
    for c in range(CHUNKS):
        for r in range(3):
            for k in range(2):
                at = c * CW + (k * 3 + r) * HEAD
                chunk_s[c * TOK:(c + 1) * TOK, (2 * r + k) * HEAD:(2 * r + k + 1) * HEAD] = (
                    q_in[:, at:at + HEAD]
                )
    q8[g] = chunk_s[...].astype(bf16)
    kv_in = kv_ref[...].astype(f32)
    for c in range(CHUNKS):
        chunk_s[c * TOK:(c + 1) * TOK, 0:128] = kv_in[:, c * 128:(c + 1) * 128]
        chunk_s[c * TOK:(c + 1) * TOK, 128:256] = kv_in[:, 512 + c * 128:512 + (c + 1) * 128]
    r8[g, :, 0:256] = chunk_s[:, 0:256].astype(bf16)
    res_in = res_ref[...].astype(f32)
    for c in range(CHUNKS):
        chunk_s[c * TOK:(c + 1) * TOK, :] = res_in[:, c * CW:(c + 1) * CW]
    r8[g, :, 256:640] = chunk_s[...].astype(bf16)

    def q8_copy(k, source):
        return pltpu.make_async_remote_copy(
            src_ref=q8.at[source], dst_ref=q8.at[source], send_sem=s_q8.at[k],
            recv_sem=r_q8.at[source], device_id={"req": req_peer(k)}, device_id_type=MESH,
        )

    def r8_copy(k, source):
        return pltpu.make_async_remote_copy(
            src_ref=r8.at[source], dst_ref=r8.at[source], send_sem=s_r8.at[k],
            recv_sem=r_r8.at[source], device_id={"req": req_peer(k)}, device_id_type=MESH,
        )

    def q_copy(k, source):
        return pltpu.make_async_remote_copy(
            src_ref=qall.at[source], dst_ref=qall.at[source], send_sem=s_q.at[k],
            recv_sem=r_q.at[source], device_id={"tp": tp_peer(k)}, device_id_type=MESH,
        )

    def kv_copy(k, source):
        return pltpu.make_async_remote_copy(
            src_ref=kvall.at[source], dst_ref=kvall.at[source], send_sem=s_kv.at[k],
            recv_sem=r_kv.at[source], device_id={"tp": slot_peer(k)}, device_id_type=MESH,
        )

    def o_copy(k, block, source):
        return pltpu.make_async_remote_copy(
            src_ref=osend.at[block], dst_ref=orecv.at[source], send_sem=s_o.at[k],
            recv_sem=r_o.at[source], device_id={"tp": tp_peer(k)}, device_id_type=MESH,
        )

    def n_copy(k, source):
        return pltpu.make_async_remote_copy(
            src_ref=nall.at[source], dst_ref=nall.at[source], send_sem=s_n.at[k],
            recv_sem=r_n.at[source], device_id={"tp": tp_peer(k)}, device_id_type=MESH,
        )

    def m_copy(k, block, source):
        return pltpu.make_async_remote_copy(
            src_ref=msend.at[block], dst_ref=mrecv.at[source], send_sem=s_m.at[k],
            recv_sem=r_m.at[source], device_id={"tp": tp_peer(k)}, device_id_type=MESH,
        )

    def each(count, step):
        def body(k, carry):
            step(k)
            return carry

        lax.fori_loop(1, count, body, 0)

    row_a = iota((256, 256), 0)
    row_b = iota((256, 256), 1)
    perm_s[...] = ones_at(
        row_b == ((row_a & 63) >> 2) * ROWS + (row_a >> 6) * TOK + (row_a & 3)
    )
    permt_s[...] = ones_at(
        row_a == ((row_b & 63) >> 2) * ROWS + (row_b >> 6) * TOK + (row_b & 3)
    )

    pl.semaphore_wait(barrier, N_REQ - 1 + N_TP - 1)

    each(N_REQ, lambda k: q8_copy(k, g).start())
    each(N_REQ, lambda k: r8_copy(k, g).start())

    node_m = iota((DRAFT, DRAFT), 0)
    node_n = iota((DRAFT, DRAFT), 1)
    parent_row = par_ref[pl.ds(half, 1), :]
    reach_t = ones_at(((node_m == parent_row) & (node_n > 0)) | (node_m == node_n))
    for _ in range(6):
        reach_t = jnp.minimum(dot(reach_t, reach_t), 1.0).astype(bf16)
    own_node = t_in * TOK + (iota((ROWS, DRAFT), 0) & 3)
    lane_node = iota((ROWS, DRAFT), 1)
    spread_row = iota((DRAFT, 256), 0)
    spread_lane = iota((DRAFT, 256), 1)
    spread = ones_at(spread_row == (spread_lane >> 4) * TOK + (spread_lane & 3))
    same_chunk = ((iota((ROWS, 256), 1) >> 2) & 3) == (iota((ROWS, 256), 0) >> 2)
    own_reach = dot_t(ones_at(lane_node == own_node), reach_t).astype(bf16)
    tree_mask = jnp.where(same_chunk, dot(own_reach, spread), 0.0)
    flags = dot_t(ones_at(lane_node == leaf[half]), reach_t)
    rank = dot(flags.astype(bf16), ones_at(node_m <= node_n)) - 1.0
    chosen = ones_at((flags > 0.5) & (rank == own_node.astype(f32)))
    choice = jnp.where(same_chunk, dot(chosen, spread), 0.0).astype(bf16)

    lane_one = iota((1, 128), 1)
    lo = ones_at(lane_one < HEAD)
    hi = ones_at(lane_one >= HEAD)

    each(N_REQ, lambda k: q8_copy(k, req_peer(k)).wait_recv())
    source_group = lax.shift_right_logical(placement[half], 1)
    own_q = q8[source_group]
    qall[t] = own_q
    each(N_TP, lambda k: q_copy(k, t).start())
    each(N_REQ, lambda k: r8_copy(k, req_peer(k)).wait_recv())
    own_kvres = r8[source_group]
    kvall[t_in] = own_kvres[:, 0:256]
    each(HALF, lambda k: kv_copy(k, t_in).start())
    own_res = own_kvres[:, 256:640].astype(f32)
    for c in range(CHUNKS):
        res_s[0:TOK, c * CW:(c + 1) * CW] = own_res[c * TOK:(c + 1) * TOK, :]

    ones_page = two_ones(PAGE)
    loads[0].wait()
    loads[1].wait()
    each(N_TP, lambda k: q_copy(k, tp_peer(k)).wait_recv())
    stat_lane = iota((DRAFT, 128), 1)
    piece = stat_lane & 7
    stat_r = (stat_lane & 63) >> 3
    for s in range(2):
        q_slot = dot(perm_s[...], qall[s * HALF:(s + 1) * HALF].reshape(256, CW)).astype(bf16)
        page = table[s]
        page_k = kbuf[page]
        page_v = vbuf[page]
        valid = t * PAGE + iota((1, PAGE), 1) < lengths[s]
        for c in range(CHUNKS):
            q_c = q_slot[c * DRAFT:(c + 1) * DRAFT]
            stacked = jnp.concatenate([q_c[:, r * 128:(r + 1) * 128] for r in range(3)], axis=0)
            out, lse = softmax_block(
                stacked, page_k[:, c * 128:(c + 1) * 128], page_v[:, c * 128:(c + 1) * 128],
                lo, hi, ones_page, valid,
            )
            stats = jnp.zeros((DRAFT, 128), f32)
            for r in range(3):
                outs_s[c * DRAFT:(c + 1) * DRAFT, r * 128:(r + 1) * 128] = (
                    out[r * DRAFT:(r + 1) * DRAFT].astype(bf16)
                )
                part = lse[r * DRAFT:(r + 1) * DRAFT]
                first = part.astype(bf16).astype(f32)
                rest = part - first
                second = rest.astype(bf16).astype(f32)
                third = rest - second
                value = jnp.where(piece == 0, first, jnp.where(piece == 1, second, third))
                stats = jnp.where((stat_r == r) & (piece < 3), value, stats)
            outs_s[c * DRAFT:(c + 1) * DRAFT, CW:512] = stats.astype(bf16)
        osend[s * HALF:(s + 1) * HALF] = (
            dot(permt_s[...], outs_s[...]).astype(bf16).reshape(HALF, ROWS, 512)
        )

    each(N_TP, lambda k: o_copy(k, tp_peer(k), t).start())
    orecv[t] = osend[t]

    each(HALF, lambda k: kv_copy(k, lax.rem(t_in + k, HALF)).wait_recv())
    kv_slot = kvall[...].reshape(256, 256)
    accepted = dot(choice, kv_slot)
    for c in range(CHUNKS):
        acc_ref[:, c * 128:(c + 1) * 128] = accepted[c * TOK:(c + 1) * TOK, 0:128].astype(bf16)
        acc_ref[:, 512 + c * 128:512 + (c + 1) * 128] = (
            accepted[c * TOK:(c + 1) * TOK, 128:256].astype(bf16)
        )
    q_own = jnp.concatenate([own_q[:, r * 128:(r + 1) * 128] for r in range(3)], axis=0)
    tree_valid = jnp.concatenate([tree_mask] * 3, axis=0) > 0.5
    tree_out, tree_lse = softmax_block(
        q_own, kv_slot[:, 0:128], kv_slot[:, 128:256], lo, hi, two_ones(256), tree_valid
    )
    tree_out = jnp.concatenate([tree_out[r * ROWS:(r + 1) * ROWS] for r in range(3)], axis=1)
    tree_lse = jnp.concatenate([tree_lse[r * ROWS:(r + 1) * ROWS] for r in range(3)], axis=1)
    ex_l = iota((128, CW), 0)
    ex_c = iota((128, CW), 1)
    expand = ones_at(
        ((ex_l >> 6) == ((ex_c >> 6) & 1)) & (((ex_l & 63) >> 3) == (ex_c >> 7)) & ((ex_l & 7) < 3)
    )

    each(N_TP, lambda k: o_copy(k, 0, tp_peer(k)).wait_recv())
    lse_all = dot(orecv[:, :, CW:512].reshape(N_TP * ROWS, 128), expand).reshape(N_TP, ROWS, CW)
    top = jnp.maximum(jnp.max(lse_all, axis=0), tree_lse)
    scale = jnp.exp(lse_all - top[None])
    tree_scale = jnp.exp(tree_lse - top)
    total = jnp.sum(scale, axis=0) + tree_scale
    joined = jnp.sum(scale * orecv[:, :, 0:CW].astype(f32), axis=0) + tree_scale * tree_out
    joined = joined / total
    for c in range(CHUNKS):
        for r in range(3):
            for k in range(2):
                at = c * CW + (k * 3 + r) * HEAD
                flat_s[0:TOK, at:at + HEAD] = (
                    joined[c * TOK:(c + 1) * TOK, (2 * r + k) * HEAD:(2 * r + k + 1) * HEAD]
                )
    attn = flat_s[0:TOK, :].astype(bf16)
    attn_ref[...] = attn

    loads[2].wait()
    hidden = res_s[0:TOK, :] + dot(attn, ow[...])
    mean = jnp.mean(hidden * hidden, axis=-1, keepdims=True)
    normed = (hidden * lax.rsqrt(mean + norm_eps) * gain_ref[...]).astype(bf16).astype(f32)
    for c in range(CHUNKS):
        chunk_s[c * TOK:(c + 1) * TOK, :] = normed[:, c * CW:(c + 1) * CW]
    nall[t] = chunk_s[...].astype(bf16)

    each(N_TP, lambda k: n_copy(k, t).start())
    expert_lane = iota((GROUP, EXPERTS), 1)
    ids = ids_ref[...]
    picked = expert_lane == ids[:, 0:1]
    for k in range(1, ids.shape[1]):
        picked = picked | (expert_lane == ids[:, k:k + 1])
    loads[3].wait()
    loads[4].wait()
    loads[5].wait()
    each(N_TP, lambda k: n_copy(k, tp_peer(k)).wait_recv())
    for s in range(2):
        rows = dot(perm_s[...], nall[s * HALF:(s + 1) * HALF].reshape(256, CW)).astype(bf16)
        for c in range(CHUNKS):
            nfull[s * DRAFT:(s + 1) * DRAFT, c * CW:(c + 1) * CW] = rows[c * DRAFT:(c + 1) * DRAFT]
    normed_all = nfull[...]
    expo = jnp.where(picked, jnp.exp(dot(normed_all, rw[...])), 0.0)
    routing = expo / jnp.sum(expo, axis=1, keepdims=True)
    for u in range(UNITS_DEV):
        expert = (t * UNITS_DEV + u) // (FF_E // UNIT)
        share = jnp.sum(jnp.where(expert_lane == expert, routing, 0.0), axis=1, keepdims=True)
        both = dot(normed_all, gu[u])
        gate = both[:, :UNIT]
        active = gate / (1.0 + jnp.exp(-gate)) * both[:, UNIT:] * share
        act_s[:, u * UNIT:(u + 1) * UNIT] = active.astype(bf16)
    moe = dot(act_s[...], dw[...].reshape(UNITS_DEV * UNIT, D)).astype(bf16)
    for s in range(2):
        for c in range(CHUNKS):
            moe_s[c * DRAFT:(c + 1) * DRAFT, :] = moe[s * DRAFT:(s + 1) * DRAFT, c * CW:(c + 1) * CW]
        msend[s * HALF:(s + 1) * HALF] = (
            dot(permt_s[...], moe_s[...]).astype(bf16).reshape(HALF, ROWS, CW)
        )

    each(N_TP, lambda k: m_copy(k, tp_peer(k), t).start())
    mrecv[t] = msend[t]
    each(N_REQ, lambda k: q8_copy(k, g).wait_send())
    each(N_REQ, lambda k: r8_copy(k, g).wait_send())
    each(N_TP, lambda k: q_copy(k, t).wait_send())
    each(HALF, lambda k: kv_copy(k, t_in).wait_send())
    each(N_TP, lambda k: o_copy(k, 0, t).wait_send())
    each(N_TP, lambda k: n_copy(k, t).wait_send())
    each(N_TP, lambda k: m_copy(k, 0, tp_peer(k)).wait_recv())
    moe_own = jnp.sum(mrecv[...].astype(f32), axis=0)
    for c in range(CHUNKS):
        flat_s[0:TOK, c * CW:(c + 1) * CW] = moe_own[c * TOK:(c + 1) * TOK, :]
    layer_ref[...] = (hidden + flat_s[0:TOK, :]).astype(bf16)
    each(N_TP, lambda k: m_copy(k, 0, t).wait_send())


def per_device(
    queries, new_kv, residual, placement, lengths, page_table, cache_keys, cache_values,
    parents, accept_leaf, out_weight, norm_gain, router_weight, expert_ids, gate_up, down_weight,
):
    smem = pl.BlockSpec(memory_space=pltpu.SMEM)
    vmem = pl.BlockSpec(memory_space=pltpu.VMEM)
    hbm = pl.BlockSpec(memory_space=pl.ANY)
    dma = pltpu.SemaphoreType.DMA
    return pl.pallas_call(
        kernel,
        out_shape=(
            jax.ShapeDtypeStruct((TOK, D), bf16),
            jax.ShapeDtypeStruct((TOK, D), bf16),
            jax.ShapeDtypeStruct((TOK, 1024), bf16),
        ),
        in_specs=[smem] * 4 + [vmem] * 6 + [hbm] * 6,
        out_specs=(vmem, vmem, vmem),
        scratch_shapes=[
            pltpu.VMEM((2, PAGE, 512), bf16),
            pltpu.VMEM((2, PAGE, 512), bf16),
            pltpu.VMEM((D, D), bf16),
            pltpu.VMEM((D, EXPERTS), bf16),
            pltpu.VMEM((UNITS_DEV, D, 2 * UNIT), bf16),
            pltpu.VMEM((UNITS_DEV, UNIT, D), bf16),
            pltpu.VMEM((N_REQ, ROWS, CW), bf16),
            pltpu.VMEM((N_REQ, ROWS, 640), bf16),
            pltpu.VMEM((N_TP, ROWS, CW), bf16),
            pltpu.VMEM((HALF, ROWS, 256), bf16),
            pltpu.VMEM((N_TP, ROWS, 512), bf16),
            pltpu.VMEM((N_TP, ROWS, 512), bf16),
            pltpu.VMEM((N_TP, ROWS, CW), bf16),
            pltpu.VMEM((N_TP, ROWS, CW), bf16),
            pltpu.VMEM((N_TP, ROWS, CW), bf16),
            pltpu.VMEM((ROWS, CW), f32),
            pltpu.VMEM((8, D), f32),
            pltpu.VMEM((8, D), f32),
            pltpu.VMEM((256, 256), bf16),
            pltpu.VMEM((256, 256), bf16),
            pltpu.VMEM((256, 512), bf16),
            pltpu.VMEM((GROUP, D), bf16),
            pltpu.VMEM((GROUP, UNITS_DEV * UNIT), bf16),
            pltpu.VMEM((256, CW), bf16),
            dma((6,)),
            dma((N_REQ,)), dma((N_REQ,)), dma((N_REQ,)), dma((N_REQ,)),
            dma((N_TP,)), dma((N_TP,)), dma((HALF,)), dma((HALF,)),
            dma((N_TP,)), dma((N_TP,)), dma((N_TP,)), dma((N_TP,)), dma((N_TP,)), dma((N_TP,)),
        ],
        compiler_params=pltpu.CompilerParams(
            collective_id=0, has_side_effects=True, vmem_limit_bytes=48 << 20
        ),
        name="verify_layer",
    )(
        placement, lengths, page_table.reshape(2), accept_leaf,
        queries, new_kv, residual, parents, norm_gain.reshape(1, D), expert_ids,
        cache_keys, cache_values, out_weight, router_weight, gate_up, down_weight,
    )


def solution(mesh):
    in_specs = (
        P(("req", "tp"), None),
        P(("req", "tp"), None),
        P(("req", "tp"), None),
        P("req"),
        P("req"),
        P("req", None, "tp"),
        P(("req", "tp"), None, None),
        P(("req", "tp"), None, None),
        P("req", None),
        P("req"),
        P(),
        P(),
        P(),
        P("req", None),
        P("tp", None, None),
        P("tp", None, None),
    )
    out_specs = (P(("req", "tp"), None), P(("req", "tp"), None), P(("req", "tp"), None))
    return jax.shard_map(
        per_device, mesh=mesh, in_specs=in_specs, out_specs=out_specs, check_vma=False
    )
```

time: 741 us -> 88.3 us (0.12)
  blocking collectives: 291 us -> 0 us
  waiting for transfers between devices: 205 us -> 0 us
  other arithmetic: 128 us -> 0 us
  Pallas kernels: 0 us -> 72.9 us
  local copies, waits for them, and re-layouts: 79.6 us -> 13.3 us
  between operations: 15.4 us -> 0.67 us
  matrix products: 14.5 us -> 0 us
    all_gather x8 -> x0, blocking collectives: 291 us -> none  [the longest x2 105 us: joined_2(): gathered = jax.tree.map(lambda a: lax.all_gather(a, axis), part)]
    unnamed x3 -> x0, waiting for transfers between devices: 144 us -> none
    add x64 -> x0, other arithmetic: 113 us -> none  [the longest x32 70.1 us: combine_stats(): left_out.reshape(row_count, head_count, -1) * left_scale[..., None]]
    pallas_call x0 -> x1, Pallas kernels: none -> 72.9 us  [per_device(): pl.pallas_call(kernel, out_shape=(jax.ShapeDtypeStruct((TOK, D), bf16), j...]
    all_gather x1 -> x0, waiting for transfers between devices: 61.4 us -> none  [joined_2(): gathered = jax.tree.map(lambda a: lax.all_gather(a, axis), part)]
    dynamic_slice x66 -> x0, local copies, waits for them, and re-layouts: 45.7 us -> none  [the longest x62 44.7 us: take(): lax.dynamic_index_in_dim(a, source, 0, False)]
    dot_general x18 -> x0, matrix products: 14.5 us -> none  [the longest x1 3.17 us: project_rows(): jnp.dot(attn_rows, out_weight, preferred_element_type=jnp.float32)]
    unnamed x77 -> x27, local copies, waits for them, and re-layouts: 1.46 us -> 12.6 us
  transfers between devices with their start and end apart: 2 -> 0, of which waited for: 2 -> 0; matrix products, arithmetic and copies ran while one was open for 1% -> 0% of each run, Pallas kernels for 0% -> 0%
where the time goes in v1:
time: 88.3 us; the launch traced here: 86.8 us
  Pallas kernels  72.9 us (83%)
  local copies, waits for them, and re-layouts  13.3 us (15%)
    pallas_call x1, Pallas kernels, per_device(): pl.pallas_call(kernel, out_shape=(jax.ShapeDtypeStruct((TOK, D), bf16), j...  72.9 us
    unnamed x27, local copies, waits for them, and re-layouts  12.6 us

profile of v1, /device:TPU:2, one launch (start us, length us, event | category | flops | bytes accessed | tf_op | source)
XLA Modules:
  0.0 86.8 jit_solution(7436262914927532773)
XLA Ops:
  0.6 0.7 reshape.13.gain_ref
  1.3 0.8 copy.19.ids_ref
  2.1 1.1 %copy.20.rw_hbm = bf16[1536,40]{1,0:T(8,128)(2,1)S(1)} copy(bf16[1536,40]{0,1:T(8,128)(2,1)} %param.28) | data formatting | bytes 245760 | tf_op args[12]
  3.2 0.0 copy-start
  3.3 1.5 %copy-done = bf16[5,128,1536]{2,1,0:T(8,128)(2,1)S(1)} copy-done((bf16[5,128,1536]{2,1,0:T(8,128)(2,1)S(1)}, bf16[5,128,1536]{2,1,0:T(8,128)(2,1)}, u32[]{:S(2)}) %copy-start) | copy-done | bytes 1966104
  4.8 0.0 copy-start.1
  4.8 0.9 %copy-done.1 = bf16[2,128,512]{2,1,0:T(8,128)(2,1)S(1)} copy-done((bf16[2,128,512]{2,1,0:T(8,128)(2,1)S(1)}, bf16[2,128,512]{2,1,0:T(8,128)(2,1)}, u32[]{:S(2)}) %copy-start.1) | copy-done | bytes 262168
  5.7 0.0 copy-start.2
  5.8 0.9 %copy-done.2 = bf16[2,128,512]{2,1,0:T(8,128)(2,1)S(1)} copy-done((bf16[2,128,512]{2,1,0:T(8,128)(2,1)S(1)}, bf16[2,128,512]{2,1,0:T(8,128)(2,1)}, u32[]{:S(2)}) %copy-start.2) | copy-done | bytes 262168
  6.7 0.0 copy-start.3
  6.7 0.7 copy-done.3
  7.4 0.0 copy-start.4
  7.4 0.7 copy-done.4
  8.1 0.0 copy-start.5
  8.1 0.7 copy-done.5
  8.8 0.0 copy-start.6
  8.8 0.7 copy-done.6
  9.5 0.0 copy-start.7
  9.5 0.7 copy-done.7
  10.1 0.0 copy-start.8
  10.1 0.7 copy-done.8
  10.8 0.0 copy-start.9
  10.8 0.7 copy-done.9
  11.5 0.0 copy-start.10
  11.5 0.7 copy-done.10
  12.1 72.9 %verify_layer.1 = (bf16[4,1536]{1,0:T(4,128)(2,1)S(1)}, bf16[4,1536]{1,0:T(4,128)(2,1)S(1)}, bf16[4,1024]{1,0:T(4,128)(2,1)S(1)}) custom-call(s32[2]{0:T(128)S(1)} %copy-done.7, s32[2]{0:T(128)S(1)} %copy-done.8, s32[2]{0:T(128)S(1)} %bitcast.1, s32[2]{0:T(128)S(1)} %copy-done.10, bf16[4,1536]{1,0:T(4,128)(2,1)S(1)} %copy-done.3, ...), custom_call_target="tpu_custom_call" | custom-call | tf_op jit(solution)/shard_map/verify_layer/pallas_call | solution.py:385
  85.0 0.6 copy.24
  85.6 0.6 copy.25
  86.2 0.6 copy.26
Async XLA Ops:
  3.2 1.5 %copy-start = (bf16[5,128,1536]{2,1,0:T(8,128)(2,1)S(1)}, bf16[5,128,1536]{2,1,0:T(8,128)(2,1)}, u32[]{:S(2)}) copy-start(bf16[5,128,1536]{2,1,0:T(8,128)(2,1)} %dw_hbm.1) | copy-start | bytes 5898244
  4.8 0.9 %copy-start.1 = (bf16[2,128,512]{2,1,0:T(8,128)(2,1)S(1)}, bf16[2,128,512]{2,1,0:T(8,128)(2,1)}, u32[]{:S(2)}) copy-start(bf16[2,128,512]{2,1,0:T(8,128)(2,1)} %keys_hbm.1) | copy-start | bytes 786436
  5.7 0.9 %copy-start.2 = (bf16[2,128,512]{2,1,0:T(8,128)(2,1)S(1)}, bf16[2,128,512]{2,1,0:T(8,128)(2,1)}, u32[]{:S(2)}) copy-start(bf16[2,128,512]{2,1,0:T(8,128)(2,1)} %vals_hbm.1) | copy-start | bytes 786436
  6.7 0.7 copy-start.3
  7.4 0.7 copy-start.4
  8.1 0.7 copy-start.5
  8.8 0.7 copy-start.6
  9.5 0.7 copy-start.7
  10.1 0.7 copy-start.8
  10.8 0.7 copy-start.9
  11.5 0.7 copy-start.10

commit v2 on v1

--- a/solution.py
+++ b/solution.py
@@ -76,11 +76,11 @@
 
 
 def kernel(
-    placement, lengths, table, leaf,
-    q_ref, kv_ref, res_ref, par_ref, gain_ref, ids_ref,
-    keys_hbm, vals_hbm, ow_hbm, rw_hbm, gu_hbm, dw_hbm,
+    q_hbm, kv_hbm, res_hbm, placement_hbm, lengths_hbm, table_hbm, keys_hbm, vals_hbm,
+    par_hbm, leaf_hbm, ow_hbm, gain_hbm, rw_hbm, ids_hbm, gu_hbm, dw_hbm,
     attn_ref, layer_ref, acc_ref,
-    kbuf, vbuf, ow, rw, gu, dw,
+    q_ref, kv_ref, res_ref, placement, lengths, table, kbuf, vbuf,
+    par_ref, leaf, ow, gain_ref, rw, ids_ref, gu, dw,
     q8, r8, qall, kvall, osend, orecv, nall, msend, mrecv,
     chunk_s, flat_s, res_s, perm_s, permt_s, outs_s, nfull, act_s, moe_s,
     wsem, s_q8, r_q8, s_r8, r_r8, s_q, r_q, s_kv, r_kv, s_o, r_o, s_n, r_n, s_m, r_m,
@@ -109,18 +109,31 @@
         pl.semaphore_signal(barrier, inc=1, device_id={"tp": tp_peer(k)}, device_id_type=MESH)
         return carry
 
+    def load(i, source, target):
+        copy = pltpu.make_async_copy(source, target, wsem.at[i])
+        copy.start()
+        return copy
+
+    load_q = load(0, q_hbm, q_ref)
+    load_kv = load(1, kv_hbm, kv_ref)
+    load_res = load(2, res_hbm, res_ref)
     lax.fori_loop(1, N_REQ, greet_req, 0)
     lax.fori_loop(1, N_TP, greet_tp, 0)
-
-    loads = [
-        pltpu.make_async_copy(a, b, wsem.at[i])
-        for i, (a, b) in enumerate(
-            [(keys_hbm, kbuf), (vals_hbm, vbuf), (ow_hbm, ow), (rw_hbm, rw), (gu_hbm, gu), (dw_hbm, dw)]
-        )
-    ]
-    for load in loads:
-        load.start()
-
+    load_placement = load(3, placement_hbm, placement)
+    load_par = load(4, par_hbm, par_ref)
+    load_leaf = load(5, leaf_hbm, leaf)
+    load_lengths = load(6, lengths_hbm, lengths)
+    load_table = load(7, table_hbm, table)
+    load_keys = load(8, keys_hbm, kbuf)
+    load_vals = load(9, vals_hbm, vbuf)
+    load_gain = load(10, gain_hbm, gain_ref.at[0])
+    load_ids = load(11, ids_hbm, ids_ref)
+    load_rw = load(12, rw_hbm, rw)
+    load_ow = load(13, ow_hbm, ow)
+    load_gu = load(14, gu_hbm, gu)
+    load_dw = load(15, dw_hbm, dw)
+
+    load_q.wait()
     q_in = q_ref[...].astype(f32) * (HEAD ** -0.5)
     for c in range(CHUNKS):
         for r in range(3):
@@ -130,11 +143,13 @@
                     q_in[:, at:at + HEAD]
                 )
     q8[g] = chunk_s[...].astype(bf16)
+    load_kv.wait()
     kv_in = kv_ref[...].astype(f32)
     for c in range(CHUNKS):
         chunk_s[c * TOK:(c + 1) * TOK, 0:128] = kv_in[:, c * 128:(c + 1) * 128]
         chunk_s[c * TOK:(c + 1) * TOK, 128:256] = kv_in[:, 512 + c * 128:512 + (c + 1) * 128]
     r8[g, :, 0:256] = chunk_s[:, 0:256].astype(bf16)
+    load_res.wait()
     res_in = res_ref[...].astype(f32)
     for c in range(CHUNKS):
         chunk_s[c * TOK:(c + 1) * TOK, :] = res_in[:, c * CW:(c + 1) * CW]
@@ -205,6 +220,8 @@
 
     node_m = iota((DRAFT, DRAFT), 0)
     node_n = iota((DRAFT, DRAFT), 1)
+    load_par.wait()
+    load_leaf.wait()
     parent_row = par_ref[pl.ds(half, 1), :]
     reach_t = ones_at(((node_m == parent_row) & (node_n > 0)) | (node_m == node_n))
     for _ in range(6):
@@ -227,6 +244,7 @@
     hi = ones_at(lane_one >= HEAD)
 
     each(N_REQ, lambda k: q8_copy(k, req_peer(k)).wait_recv())
+    load_placement.wait()
     source_group = lax.shift_right_logical(placement[half], 1)
     own_q = q8[source_group]
     qall[t] = own_q
@@ -240,8 +258,10 @@
         res_s[0:TOK, c * CW:(c + 1) * CW] = own_res[c * TOK:(c + 1) * TOK, :]
 
     ones_page = two_ones(PAGE)
-    loads[0].wait()
-    loads[1].wait()
+    load_lengths.wait()
+    load_table.wait()
+    load_keys.wait()
+    load_vals.wait()
     each(N_TP, lambda k: q_copy(k, tp_peer(k)).wait_recv())
     stat_lane = iota((DRAFT, 128), 1)
     piece = stat_lane & 7
@@ -318,7 +338,8 @@
     attn = flat_s[0:TOK, :].astype(bf16)
     attn_ref[...] = attn
 
-    loads[2].wait()
+    load_ow.wait()
+    load_gain.wait()
     hidden = res_s[0:TOK, :] + dot(attn, ow[...])
     mean = jnp.mean(hidden * hidden, axis=-1, keepdims=True)
     normed = (hidden * lax.rsqrt(mean + norm_eps) * gain_ref[...]).astype(bf16).astype(f32)
@@ -327,25 +348,36 @@
     nall[t] = chunk_s[...].astype(bf16)
 
     each(N_TP, lambda k: n_copy(k, t).start())
-    expert_lane = iota((GROUP, EXPERTS), 1)
+    expert_row = iota((EXPERTS, GROUP), 0)
+    load_ids.wait()
     ids = ids_ref[...]
-    picked = expert_lane == ids[:, 0:1]
-    for k in range(1, ids.shape[1]):
-        picked = picked | (expert_lane == ids[:, k:k + 1])
-    loads[3].wait()
-    loads[4].wait()
-    loads[5].wait()
+    picked = expert_row == ids[0:1]
+    for k in range(1, ids.shape[0]):
+        picked = picked | (expert_row == ids[k:k + 1])
+    load_rw.wait()
+    load_gu.wait()
+    load_dw.wait()
     each(N_TP, lambda k: n_copy(k, tp_peer(k)).wait_recv())
     for s in range(2):
         rows = dot(perm_s[...], nall[s * HALF:(s + 1) * HALF].reshape(256, CW)).astype(bf16)
         for c in range(CHUNKS):
             nfull[s * DRAFT:(s + 1) * DRAFT, c * CW:(c + 1) * CW] = rows[c * DRAFT:(c + 1) * DRAFT]
     normed_all = nfull[...]
-    expo = jnp.where(picked, jnp.exp(dot(normed_all, rw[...])), 0.0)
-    routing = expo / jnp.sum(expo, axis=1, keepdims=True)
+    expo = jnp.where(picked, jnp.exp(dot_t(rw[...], normed_all)), 0.0)
+    routing = expo / jnp.sum(expo, axis=0, keepdims=True)
+    first_expert = t * UNITS_DEV // (FF_E // UNIT)
+    two = jnp.concatenate(
+        [
+            jnp.sum(jnp.where(expert_row == first_expert + k, routing, 0.0), axis=0, keepdims=True)
+            for k in range(2)
+        ]
+        + [jnp.zeros((GROUP - 2, GROUP), f32)],
+        axis=0,
+    )
+    columns = jnp.transpose(two)
     for u in range(UNITS_DEV):
-        expert = (t * UNITS_DEV + u) // (FF_E // UNIT)
-        share = jnp.sum(jnp.where(expert_lane == expert, routing, 0.0), axis=1, keepdims=True)
+        same = (t * UNITS_DEV + u) // (FF_E // UNIT) == first_expert
+        share = jnp.where(same, columns[:, 0:1], columns[:, 1:2])
         both = dot(normed_all, gu[u])
         gate = both[:, :UNIT]
         active = gate / (1.0 + jnp.exp(-gate)) * both[:, UNIT:] * share
@@ -378,9 +410,8 @@
     queries, new_kv, residual, placement, lengths, page_table, cache_keys, cache_values,
     parents, accept_leaf, out_weight, norm_gain, router_weight, expert_ids, gate_up, down_weight,
 ):
-    smem = pl.BlockSpec(memory_space=pltpu.SMEM)
     vmem = pl.BlockSpec(memory_space=pltpu.VMEM)
-    hbm = pl.BlockSpec(memory_space=pl.ANY)
+    hbm = pl.BlockSpec(memory_space=pltpu.MemorySpace.HBM)
     dma = pltpu.SemaphoreType.DMA
     return pl.pallas_call(
         kernel,
@@ -389,13 +420,23 @@
             jax.ShapeDtypeStruct((TOK, D), bf16),
             jax.ShapeDtypeStruct((TOK, 1024), bf16),
         ),
-        in_specs=[smem] * 4 + [vmem] * 6 + [hbm] * 6,
+        in_specs=[hbm] * 16,
         out_specs=(vmem, vmem, vmem),
         scratch_shapes=[
+            pltpu.VMEM((TOK, D), bf16),
+            pltpu.VMEM((TOK, 1024), bf16),
+            pltpu.VMEM((TOK, D), bf16),
+            pltpu.SMEM((2,), jnp.int32),
+            pltpu.SMEM((2,), jnp.int32),
+            pltpu.SMEM((2,), jnp.int32),
             pltpu.VMEM((2, PAGE, 512), bf16),
             pltpu.VMEM((2, PAGE, 512), bf16),
+            pltpu.VMEM((2, DRAFT), jnp.int32),
+            pltpu.SMEM((2,), jnp.int32),
             pltpu.VMEM((D, D), bf16),
-            pltpu.VMEM((D, EXPERTS), bf16),
+            pltpu.VMEM((1, D), f32),
+            pltpu.VMEM((EXPERTS, D), bf16),
+            pltpu.VMEM((8, GROUP), jnp.int32),
             pltpu.VMEM((UNITS_DEV, D, 2 * UNIT), bf16),
             pltpu.VMEM((UNITS_DEV, UNIT, D), bf16),
             pltpu.VMEM((N_REQ, ROWS, CW), bf16),
@@ -416,19 +457,19 @@
             pltpu.VMEM((GROUP, D), bf16),
             pltpu.VMEM((GROUP, UNITS_DEV * UNIT), bf16),
             pltpu.VMEM((256, CW), bf16),
-            dma((6,)),
+            dma((16,)),
             dma((N_REQ,)), dma((N_REQ,)), dma((N_REQ,)), dma((N_REQ,)),
             dma((N_TP,)), dma((N_TP,)), dma((HALF,)), dma((HALF,)),
             dma((N_TP,)), dma((N_TP,)), dma((N_TP,)), dma((N_TP,)), dma((N_TP,)), dma((N_TP,)),
         ],
         compiler_params=pltpu.CompilerParams(
-            collective_id=0, has_side_effects=True, vmem_limit_bytes=48 << 20
+            collective_id=0, has_side_effects=True, vmem_limit_bytes=64 << 20
         ),
         name="verify_layer",
     )(
-        placement, lengths, page_table.reshape(2), accept_leaf,
-        queries, new_kv, residual, parents, norm_gain.reshape(1, D), expert_ids,
-        cache_keys, cache_values, out_weight, router_weight, gate_up, down_weight,
+        queries, new_kv, residual, placement, lengths, page_table.reshape(2),
+        cache_keys, cache_values, parents, accept_leaf, out_weight, norm_gain,
+        router_weight.T, expert_ids.T, gate_up, down_weight,
     )
 
 

time: 88.3 us -> 79 us (0.89)
  local copies, waits for them, and re-layouts: 13.3 us -> 3.92 us
    unnamed x27 -> x3, local copies, waits for them, and re-layouts: 12.6 us -> 3.92 us
where the time goes in v2:
time: 79 us; the launch traced here: 77.7 us
  Pallas kernels  73.1 us (93%)
  local copies, waits for them, and re-layouts  3.92 us (5%)
    pallas_call x1, Pallas kernels, per_device(): pl.pallas_call(kernel, out_shape=(jax.ShapeDtypeStruct((TOK, D), bf16), j...  73.1 us
    unnamed x3, local copies, waits for them, and re-layouts  3.92 us

profile of v2, /device:TPU:2, one launch (start us, length us, event | category | flops | bytes accessed | tf_op | source)
XLA Modules:
  0.0 77.7 jit_solution(1376141647316484119)
XLA Ops:
  0.6 73.1 %verify_layer.1 = (bf16[4,1536]{1,0:T(4,128)(2,1)}, bf16[4,1536]{1,0:T(4,128)(2,1)}, bf16[4,1024]{1,0:T(4,128)(2,1)}) custom-call(bf16[4,1536]{1,0:T(4,128)(2,1)} %q_hbm.1, bf16[4,1024]{1,0:T(4,128)(2,1)} %kv_hbm.1, bf16[4,1536]{1,0:T(4,128)(2,1)} %res_hbm.1, s32[2]{0:T(128)} %placement_hbm.1, s32[2]{0:T(128)} %lengths_hbm.1, s32[2]{0:T(128)} %bitcast.5, ...), custom_call_target="tpu_custom_call" | custom-call | tf_op jit(solution)/shard_map/verify_layer/pallas_call | solution.py:416
  73.8 1.3 %copy.22 = bf16[4,1536]{1,0:T(4,128)(2,1)} copy(bf16[4,1536]{1,0:T(4,128)(2,1)} %get-tuple-element.6) | data formatting | bytes 24576
  75.1 1.3 %copy.23 = bf16[4,1536]{1,0:T(4,128)(2,1)} copy(bf16[4,1536]{1,0:T(4,128)(2,1)} %get-tuple-element.7) | data formatting | bytes 24576
  76.4 1.3 %copy.24 = bf16[4,1024]{1,0:T(4,128)(2,1)} copy(bf16[4,1024]{1,0:T(4,128)(2,1)} %get-tuple-element.8) | data formatting | bytes 16384

commit v3 on v2

--- a/solution.py
+++ b/solution.py
@@ -81,12 +81,14 @@
     attn_ref, layer_ref, acc_ref,
     q_ref, kv_ref, res_ref, placement, lengths, table, kbuf, vbuf,
     par_ref, leaf, ow, gain_ref, rw, ids_ref, gu, dw,
-    q8, r8, qall, kvall, osend, orecv, nall, msend, mrecv,
-    chunk_s, flat_s, res_s, perm_s, permt_s, outs_s, nfull, act_s, moe_s,
-    wsem, s_q8, r_q8, s_r8, r_r8, s_q, r_q, s_kv, r_kv, s_o, r_o, s_n, r_n, s_m, r_m,
+    q8, r8, qown, qall, kvall, pages_send, pages, osend, orecv, nall, msend, mrecv,
+    heads_s, chunk_s, flat_s, res_s, perm_s, permt_s, nfull, act_s, moe_s,
+    wsem, s_p, r_p, s_q8, r_q8, s_r8, r_r8, s_q, r_q, s_kv, r_kv, s_o, r_o, s_n, r_n, s_m, r_m,
 ):
     g = lax.axis_index("req")
     t = lax.axis_index("tp")
+    x = t % 4
+    row_start = t - x
     half = t // HALF
     t_in = t % HALF
 
@@ -135,14 +137,14 @@
 
     load_q.wait()
     q_in = q_ref[...].astype(f32) * (HEAD ** -0.5)
+    heads_s[...] = jnp.zeros_like(heads_s)
     for c in range(CHUNKS):
         for r in range(3):
             for k in range(2):
                 at = c * CW + (k * 3 + r) * HEAD
-                chunk_s[c * TOK:(c + 1) * TOK, (2 * r + k) * HEAD:(2 * r + k + 1) * HEAD] = (
-                    q_in[:, at:at + HEAD]
-                )
-    q8[g] = chunk_s[...].astype(bf16)
+                row = c * ROWS + r * TOK
+                heads_s[row:row + TOK, k * HEAD:(k + 1) * HEAD] = q_in[:, at:at + HEAD]
+    q8[g] = heads_s[...].astype(bf16).reshape(CHUNKS, ROWS, 128)
     load_kv.wait()
     kv_in = kv_ref[...].astype(f32)
     for c in range(CHUNKS):
@@ -155,6 +157,13 @@
         chunk_s[c * TOK:(c + 1) * TOK, :] = res_in[:, c * CW:(c + 1) * CW]
     r8[g, :, 256:640] = chunk_s[...].astype(bf16)
 
+    def page_copy(k, source):
+        peer = lax.rem(x + k, 4)
+        return pltpu.make_async_remote_copy(
+            src_ref=pages_send.at[peer], dst_ref=pages.at[source], send_sem=s_p.at[k],
+            recv_sem=r_p.at[source], device_id={"tp": row_start + peer}, device_id_type=MESH,
+        )
+
     def q8_copy(k, source):
         return pltpu.make_async_remote_copy(
             src_ref=q8.at[source], dst_ref=q8.at[source], send_sem=s_q8.at[k],
@@ -169,7 +178,7 @@
 
     def q_copy(k, source):
         return pltpu.make_async_remote_copy(
-            src_ref=qall.at[source], dst_ref=qall.at[source], send_sem=s_q.at[k],
+            src_ref=qown.at[lax.rem(x + k % 4, 4)], dst_ref=qall.at[source], send_sem=s_q.at[k],
             recv_sem=r_q.at[source], device_id={"tp": tp_peer(k)}, device_id_type=MESH,
         )
 
@@ -217,6 +226,18 @@
 
     each(N_REQ, lambda k: q8_copy(k, g).start())
     each(N_REQ, lambda k: r8_copy(k, g).start())
+
+    load_table.wait()
+    load_keys.wait()
+    load_vals.wait()
+    for s in range(2):
+        page_k = kbuf[table[s]]
+        page_v = vbuf[table[s]]
+        for c in range(CHUNKS):
+            pages_send[c, s] = page_k[:, c * 128:(c + 1) * 128]
+            pages_send[c, 2 + s] = page_v[:, c * 128:(c + 1) * 128]
+    each(4, lambda k: page_copy(k, x).start())
+    pages[x] = pages_send[x]
 
     node_m = iota((DRAFT, DRAFT), 0)
     node_n = iota((DRAFT, DRAFT), 1)
@@ -228,12 +249,15 @@
         reach_t = jnp.minimum(dot(reach_t, reach_t), 1.0).astype(bf16)
     own_node = t_in * TOK + (iota((ROWS, DRAFT), 0) & 3)
     lane_node = iota((ROWS, DRAFT), 1)
+    tree_node = t_in * TOK + (iota((CHUNKS * ROWS, DRAFT), 0) & 3)
+    tree_lane = iota((CHUNKS * ROWS, DRAFT), 1)
     spread_row = iota((DRAFT, 256), 0)
     spread_lane = iota((DRAFT, 256), 1)
     spread = ones_at(spread_row == (spread_lane >> 4) * TOK + (spread_lane & 3))
     same_chunk = ((iota((ROWS, 256), 1) >> 2) & 3) == (iota((ROWS, 256), 0) >> 2)
-    own_reach = dot_t(ones_at(lane_node == own_node), reach_t).astype(bf16)
-    tree_mask = jnp.where(same_chunk, dot(own_reach, spread), 0.0)
+    tree_chunk = ((iota((CHUNKS * ROWS, 256), 1) >> 2) & 3) == (iota((CHUNKS * ROWS, 256), 0) >> 4)
+    own_reach = dot_t(ones_at(tree_lane == tree_node), reach_t).astype(bf16)
+    tree_valid = jnp.where(tree_chunk, dot(own_reach, spread), 0.0) > 0.5
     flags = dot_t(ones_at(lane_node == leaf[half]), reach_t)
     rank = dot(flags.astype(bf16), ones_at(node_m <= node_n)) - 1.0
     chosen = ones_at((flags > 0.5) & (rank == own_node.astype(f32)))
@@ -247,7 +271,8 @@
     load_placement.wait()
     source_group = lax.shift_right_logical(placement[half], 1)
     own_q = q8[source_group]
-    qall[t] = own_q
+    qown[...] = own_q
+    qall[t] = qown[x]
     each(N_TP, lambda k: q_copy(k, t).start())
     each(N_REQ, lambda k: r8_copy(k, req_peer(k)).wait_recv())
     own_kvres = r8[source_group]
@@ -257,44 +282,24 @@
     for c in range(CHUNKS):
         res_s[0:TOK, c * CW:(c + 1) * CW] = own_res[c * TOK:(c + 1) * TOK, :]
 
-    ones_page = two_ones(PAGE)
+    span = 4 * PAGE
+    ones_page = two_ones(span)
+    stat_lane = iota((256, 128), 1) & (HEAD - 1)
     load_lengths.wait()
-    load_table.wait()
-    load_keys.wait()
-    load_vals.wait()
+    each(4, lambda k: page_copy(k, lax.rem(x + k, 4)).wait_recv())
     each(N_TP, lambda k: q_copy(k, tp_peer(k)).wait_recv())
-    stat_lane = iota((DRAFT, 128), 1)
-    piece = stat_lane & 7
-    stat_r = (stat_lane & 63) >> 3
     for s in range(2):
-        q_slot = dot(perm_s[...], qall[s * HALF:(s + 1) * HALF].reshape(256, CW)).astype(bf16)
-        page = table[s]
-        page_k = kbuf[page]
-        page_v = vbuf[page]
-        valid = t * PAGE + iota((1, PAGE), 1) < lengths[s]
-        for c in range(CHUNKS):
-            q_c = q_slot[c * DRAFT:(c + 1) * DRAFT]
-            stacked = jnp.concatenate([q_c[:, r * 128:(r + 1) * 128] for r in range(3)], axis=0)
-            out, lse = softmax_block(
-                stacked, page_k[:, c * 128:(c + 1) * 128], page_v[:, c * 128:(c + 1) * 128],
-                lo, hi, ones_page, valid,
-            )
-            stats = jnp.zeros((DRAFT, 128), f32)
-            for r in range(3):
-                outs_s[c * DRAFT:(c + 1) * DRAFT, r * 128:(r + 1) * 128] = (
-                    out[r * DRAFT:(r + 1) * DRAFT].astype(bf16)
-                )
-                part = lse[r * DRAFT:(r + 1) * DRAFT]
-                first = part.astype(bf16).astype(f32)
-                rest = part - first
-                second = rest.astype(bf16).astype(f32)
-                third = rest - second
-                value = jnp.where(piece == 0, first, jnp.where(piece == 1, second, third))
-                stats = jnp.where((stat_r == r) & (piece < 3), value, stats)
-            outs_s[c * DRAFT:(c + 1) * DRAFT, CW:512] = stats.astype(bf16)
-        osend[s * HALF:(s + 1) * HALF] = (
-            dot(permt_s[...], outs_s[...]).astype(bf16).reshape(HALF, ROWS, 512)
-        )
+        valid = row_start * PAGE + iota((1, span), 1) < lengths[s]
+        out, lse = softmax_block(
+            qall[s * HALF:(s + 1) * HALF].reshape(256, 128), pages[:, s].reshape(span, 128),
+            pages[:, 2 + s].reshape(span, 128), lo, hi, ones_page, valid,
+        )
+        first = lse.astype(bf16).astype(f32)
+        rest = lse - first
+        second = rest.astype(bf16).astype(f32)
+        stats = jnp.where(stat_lane == 0, first, jnp.where(stat_lane == 1, second, rest - second))
+        osend[s * HALF:(s + 1) * HALF, :, 0:128] = out.astype(bf16).reshape(HALF, ROWS, 128)
+        osend[s * HALF:(s + 1) * HALF, :, 128:256] = stats.astype(bf16).reshape(HALF, ROWS, 128)
 
     each(N_TP, lambda k: o_copy(k, tp_peer(k), t).start())
     orecv[t] = osend[t]
@@ -307,34 +312,28 @@
         acc_ref[:, 512 + c * 128:512 + (c + 1) * 128] = (
             accepted[c * TOK:(c + 1) * TOK, 128:256].astype(bf16)
         )
-    q_own = jnp.concatenate([own_q[:, r * 128:(r + 1) * 128] for r in range(3)], axis=0)
-    tree_valid = jnp.concatenate([tree_mask] * 3, axis=0) > 0.5
     tree_out, tree_lse = softmax_block(
-        q_own, kv_slot[:, 0:128], kv_slot[:, 128:256], lo, hi, two_ones(256), tree_valid
-    )
-    tree_out = jnp.concatenate([tree_out[r * ROWS:(r + 1) * ROWS] for r in range(3)], axis=1)
-    tree_lse = jnp.concatenate([tree_lse[r * ROWS:(r + 1) * ROWS] for r in range(3)], axis=1)
-    ex_l = iota((128, CW), 0)
-    ex_c = iota((128, CW), 1)
-    expand = ones_at(
-        ((ex_l >> 6) == ((ex_c >> 6) & 1)) & (((ex_l & 63) >> 3) == (ex_c >> 7)) & ((ex_l & 7) < 3)
-    )
+        own_q.reshape(CHUNKS * ROWS, 128), kv_slot[:, 0:128], kv_slot[:, 128:256], lo, hi,
+        two_ones(256), tree_valid,
+    )
+    ex_row = iota((128, 128), 0)
+    expand = ones_at(((ex_row >> 6) == (iota((128, 128), 1) >> 6)) & ((ex_row & (HEAD - 1)) < 3))
 
     each(N_TP, lambda k: o_copy(k, 0, tp_peer(k)).wait_recv())
-    lse_all = dot(orecv[:, :, CW:512].reshape(N_TP * ROWS, 128), expand).reshape(N_TP, ROWS, CW)
+    lse_all = dot(orecv[:, :, 128:256].reshape(N_TP * ROWS, 128), expand)
+    lse_all = lse_all.reshape(N_TP // 4, CHUNKS * ROWS, 128)
+    out_all = orecv[:, :, 0:128].reshape(N_TP // 4, CHUNKS * ROWS, 128).astype(f32)
     top = jnp.maximum(jnp.max(lse_all, axis=0), tree_lse)
     scale = jnp.exp(lse_all - top[None])
     tree_scale = jnp.exp(tree_lse - top)
     total = jnp.sum(scale, axis=0) + tree_scale
-    joined = jnp.sum(scale * orecv[:, :, 0:CW].astype(f32), axis=0) + tree_scale * tree_out
-    joined = joined / total
+    joined = (jnp.sum(scale * out_all, axis=0) + tree_scale * tree_out) / total
     for c in range(CHUNKS):
         for r in range(3):
             for k in range(2):
                 at = c * CW + (k * 3 + r) * HEAD
-                flat_s[0:TOK, at:at + HEAD] = (
-                    joined[c * TOK:(c + 1) * TOK, (2 * r + k) * HEAD:(2 * r + k + 1) * HEAD]
-                )
+                row = c * ROWS + r * TOK
+                flat_s[0:TOK, at:at + HEAD] = joined[row:row + TOK, k * HEAD:(k + 1) * HEAD]
     attn = flat_s[0:TOK, :].astype(bf16)
     attn_ref[...] = attn
 
@@ -392,6 +391,7 @@
 
     each(N_TP, lambda k: m_copy(k, tp_peer(k), t).start())
     mrecv[t] = msend[t]
+    each(4, lambda k: page_copy(k, x).wait_send())
     each(N_REQ, lambda k: q8_copy(k, g).wait_send())
     each(N_REQ, lambda k: r8_copy(k, g).wait_send())
     each(N_TP, lambda k: q_copy(k, t).wait_send())
@@ -439,25 +439,29 @@
             pltpu.VMEM((8, GROUP), jnp.int32),
             pltpu.VMEM((UNITS_DEV, D, 2 * UNIT), bf16),
             pltpu.VMEM((UNITS_DEV, UNIT, D), bf16),
-            pltpu.VMEM((N_REQ, ROWS, CW), bf16),
+            pltpu.VMEM((N_REQ, CHUNKS, ROWS, 128), bf16),
             pltpu.VMEM((N_REQ, ROWS, 640), bf16),
-            pltpu.VMEM((N_TP, ROWS, CW), bf16),
+            pltpu.VMEM((CHUNKS, ROWS, 128), bf16),
+            pltpu.VMEM((N_TP, ROWS, 128), bf16),
             pltpu.VMEM((HALF, ROWS, 256), bf16),
-            pltpu.VMEM((N_TP, ROWS, 512), bf16),
-            pltpu.VMEM((N_TP, ROWS, 512), bf16),
+            pltpu.VMEM((CHUNKS, 4, PAGE, 128), bf16),
+            pltpu.VMEM((4, 4, PAGE, 128), bf16),
+            pltpu.VMEM((N_TP, ROWS, 256), bf16),
+            pltpu.VMEM((N_TP, ROWS, 256), bf16),
             pltpu.VMEM((N_TP, ROWS, CW), bf16),
             pltpu.VMEM((N_TP, ROWS, CW), bf16),
             pltpu.VMEM((N_TP, ROWS, CW), bf16),
+            pltpu.VMEM((CHUNKS * ROWS, 128), f32),
             pltpu.VMEM((ROWS, CW), f32),
             pltpu.VMEM((8, D), f32),
             pltpu.VMEM((8, D), f32),
             pltpu.VMEM((256, 256), bf16),
             pltpu.VMEM((256, 256), bf16),
-            pltpu.VMEM((256, 512), bf16),
             pltpu.VMEM((GROUP, D), bf16),
             pltpu.VMEM((GROUP, UNITS_DEV * UNIT), bf16),
             pltpu.VMEM((256, CW), bf16),
             dma((16,)),
+            dma((4,)), dma((4,)),
             dma((N_REQ,)), dma((N_REQ,)), dma((N_REQ,)), dma((N_REQ,)),
             dma((N_TP,)), dma((N_TP,)), dma((HALF,)), dma((HALF,)),
             dma((N_TP,)), dma((N_TP,)), dma((N_TP,)), dma((N_TP,)), dma((N_TP,)), dma((N_TP,)),

time: 79 us -> 69.8 us (0.88); the launches traced: 77.7 us -> 69.4 us
  Pallas kernels: 73.1 us -> 64.9 us
    pallas_call x1, Pallas kernels: 73.1 us -> 64.9 us  [per_device(): pl.pallas_call(kernel, out_shape=(jax.ShapeDtypeStruct((TOK, D), bf16), j...]
where the time goes in v3:
time: 69.8 us; the launch traced here: 69.4 us
  Pallas kernels  64.9 us (93%)
  local copies, waits for them, and re-layouts  3.92 us (6%)
    pallas_call x1, Pallas kernels, per_device(): pl.pallas_call(kernel, out_shape=(jax.ShapeDtypeStruct((TOK, D), bf16), j...  64.9 us
    unnamed x3, local copies, waits for them, and re-layouts  3.92 us

profile of v3, /device:TPU:2, one launch (start us, length us, event | category | flops | bytes accessed | tf_op | source)
XLA Modules:
  0.0 69.4 jit_solution(17547353954559330382)
XLA Ops:
  0.6 64.9 %verify_layer.1 = (bf16[4,1536]{1,0:T(4,128)(2,1)}, bf16[4,1536]{1,0:T(4,128)(2,1)}, bf16[4,1024]{1,0:T(4,128)(2,1)}) custom-call(bf16[4,1536]{1,0:T(4,128)(2,1)} %q_hbm.1, bf16[4,1024]{1,0:T(4,128)(2,1)} %kv_hbm.1, bf16[4,1536]{1,0:T(4,128)(2,1)} %res_hbm.1, s32[2]{0:T(128)} %placement_hbm.1, s32[2]{0:T(128)} %lengths_hbm.1, s32[2]{0:T(128)} %bitcast.5, ...), custom_call_target="tpu_custom_call" | custom-call | tf_op jit(solution)/shard_map/verify_layer/pallas_call | solution.py:416
  65.5 1.3 %copy.22 = bf16[4,1536]{1,0:T(4,128)(2,1)} copy(bf16[4,1536]{1,0:T(4,128)(2,1)} %get-tuple-element.6) | data formatting | bytes 24576
  66.8 1.3 %copy.23 = bf16[4,1536]{1,0:T(4,128)(2,1)} copy(bf16[4,1536]{1,0:T(4,128)(2,1)} %get-tuple-element.7) | data formatting | bytes 24576
  68.1 1.3 %copy.24 = bf16[4,1024]{1,0:T(4,128)(2,1)} copy(bf16[4,1024]{1,0:T(4,128)(2,1)} %get-tuple-element.8) | data formatting | bytes 16384

commit v4 on v3

--- a/solution.py
+++ b/solution.py
@@ -1,3 +1,5 @@
+import functools
+
 import jax
 import jax.numpy as jnp
 from jax import lax
@@ -23,6 +25,7 @@
 HALF = N_TP // 2
 ROWS = CHUNKS * TOK
 GROUP = N_TP * TOK
+FAR = (3, 5, 4)
 
 neg_big = -1e30
 norm_eps = 1e-06
@@ -81,13 +84,14 @@
     attn_ref, layer_ref, acc_ref,
     q_ref, kv_ref, res_ref, placement, lengths, table, kbuf, vbuf,
     par_ref, leaf, ow, gain_ref, rw, ids_ref, gu, dw,
-    q8, r8, qown, qall, kvall, pages_send, pages, osend, orecv, nall, msend, mrecv,
+    q8, r8, qown, qall, kvall, pages_send, pages, osend, orecv, nall, msend, mrow, msum, mrecv,
     heads_s, chunk_s, flat_s, res_s, perm_s, permt_s, nfull, act_s, moe_s,
-    wsem, s_p, r_p, s_q8, r_q8, s_r8, r_r8, s_q, r_q, s_kv, r_kv, s_o, r_o, s_n, r_n, s_m, r_m,
+    wsem, sems, far_sems, row_sems,
 ):
     g = lax.axis_index("req")
     t = lax.axis_index("tp")
     x = t % 4
+    z = t // 4
     row_start = t - x
     half = t // HALF
     t_in = t % HALF
@@ -145,6 +149,90 @@
                 row = c * ROWS + r * TOK
                 heads_s[row:row + TOK, k * HEAD:(k + 1) * HEAD] = q_in[:, at:at + HEAD]
     q8[g] = heads_s[...].astype(bf16).reshape(CHUNKS, ROWS, 128)
+    def page_copy(k, source):
+        peer = lax.rem(x + k, 4)
+        return pltpu.make_async_remote_copy(
+            src_ref=pages_send.at[peer], dst_ref=pages.at[source], send_sem=sems.at[0],
+            recv_sem=sems.at[1], device_id={"tp": row_start + peer}, device_id_type=MESH,
+        )
+
+    def q8_copy(k, source):
+        return pltpu.make_async_remote_copy(
+            src_ref=q8.at[source], dst_ref=q8.at[source], send_sem=sems.at[2],
+            recv_sem=sems.at[3], device_id={"req": req_peer(k)}, device_id_type=MESH,
+        )
+
+    def r8_copy(k, source):
+        return pltpu.make_async_remote_copy(
+            src_ref=r8.at[source], dst_ref=r8.at[source], send_sem=sems.at[4],
+            recv_sem=sems.at[5], device_id={"req": req_peer(k)}, device_id_type=MESH,
+        )
+
+    def q_copy(k, source):
+        return pltpu.make_async_remote_copy(
+            src_ref=qown.at[lax.rem(x + k % 4, 4)], dst_ref=qall.at[source], send_sem=sems.at[6],
+            recv_sem=sems.at[7], device_id={"tp": tp_peer(k)}, device_id_type=MESH,
+        )
+
+    def kv_copy(k, source):
+        return pltpu.make_async_remote_copy(
+            src_ref=kvall.at[source], dst_ref=kvall.at[source], send_sem=sems.at[8],
+            recv_sem=sems.at[9], device_id={"tp": slot_peer(k)}, device_id_type=MESH,
+        )
+
+    def o_copy(k, block, source):
+        return pltpu.make_async_remote_copy(
+            src_ref=osend.at[block], dst_ref=orecv.at[source], send_sem=sems.at[10],
+            recv_sem=sems.at[11], device_id={"tp": tp_peer(k)}, device_id_type=MESH,
+        )
+
+    def far_copy(k):
+        block = t
+        return pltpu.make_async_remote_copy(
+            src_ref=nall.at[block], dst_ref=nall.at[block], send_sem=sems.at[12],
+            recv_sem=far_sems.at[k], device_id={"tp": lax.rem(z + k, 8) * 4 + x}, device_id_type=MESH,
+        )
+
+    def n_copy(block, peer):
+        return pltpu.make_async_remote_copy(
+            src_ref=nall.at[block], dst_ref=nall.at[block], send_sem=sems.at[12],
+            recv_sem=sems.at[13], device_id={"tp": peer}, device_id_type=MESH,
+        )
+
+    def row_copy(zone, k):
+        peer = lax.rem(x + k, 4)
+        return pltpu.make_async_remote_copy(
+            src_ref=msend.at[zone * 4 + peer], dst_ref=mrow.at[zone * 4 + x], send_sem=sems.at[14],
+            recv_sem=row_sems.at[zone], device_id={"tp": row_start + peer}, device_id_type=MESH,
+        )
+
+    def zone_copy(zone):
+        return pltpu.make_async_remote_copy(
+            src_ref=msum.at[zone], dst_ref=mrecv.at[z], send_sem=sems.at[15],
+            recv_sem=sems.at[16], device_id={"tp": zone * 4 + x}, device_id_type=MESH,
+        )
+
+    def near_start(k):
+        zone = k // 4
+        far = functools.reduce(jnp.logical_or, [zone == f for f in FAR])
+
+        @pl.when(jnp.logical_not(far))
+        def _():
+            n_copy(t, tp_peer(k)).start()
+
+    def await_bytes(refs, index):
+        pltpu.make_async_copy(refs, refs, sems.at[index]).wait()
+
+    def each(count, step):
+        def body(k, carry):
+            step(k)
+            return carry
+
+        lax.fori_loop(1, count, body, 0)
+
+    pl.semaphore_wait(barrier, N_REQ - 1 + N_TP - 1)
+
+    each(N_REQ, lambda k: q8_copy(k, g).start())
     load_kv.wait()
     kv_in = kv_ref[...].astype(f32)
     for c in range(CHUNKS):
@@ -157,74 +245,6 @@
         chunk_s[c * TOK:(c + 1) * TOK, :] = res_in[:, c * CW:(c + 1) * CW]
     r8[g, :, 256:640] = chunk_s[...].astype(bf16)
 
-    def page_copy(k, source):
-        peer = lax.rem(x + k, 4)
-        return pltpu.make_async_remote_copy(
-            src_ref=pages_send.at[peer], dst_ref=pages.at[source], send_sem=s_p.at[k],
-            recv_sem=r_p.at[source], device_id={"tp": row_start + peer}, device_id_type=MESH,
-        )
-
-    def q8_copy(k, source):
-        return pltpu.make_async_remote_copy(
-            src_ref=q8.at[source], dst_ref=q8.at[source], send_sem=s_q8.at[k],
-            recv_sem=r_q8.at[source], device_id={"req": req_peer(k)}, device_id_type=MESH,
-        )
-
-    def r8_copy(k, source):
-        return pltpu.make_async_remote_copy(
-            src_ref=r8.at[source], dst_ref=r8.at[source], send_sem=s_r8.at[k],
-            recv_sem=r_r8.at[source], device_id={"req": req_peer(k)}, device_id_type=MESH,
-        )
-
-    def q_copy(k, source):
-        return pltpu.make_async_remote_copy(
-            src_ref=qown.at[lax.rem(x + k % 4, 4)], dst_ref=qall.at[source], send_sem=s_q.at[k],
-            recv_sem=r_q.at[source], device_id={"tp": tp_peer(k)}, device_id_type=MESH,
-        )
-
-    def kv_copy(k, source):
-        return pltpu.make_async_remote_copy(
-            src_ref=kvall.at[source], dst_ref=kvall.at[source], send_sem=s_kv.at[k],
-            recv_sem=r_kv.at[source], device_id={"tp": slot_peer(k)}, device_id_type=MESH,
-        )
-
-    def o_copy(k, block, source):
-        return pltpu.make_async_remote_copy(
-            src_ref=osend.at[block], dst_ref=orecv.at[source], send_sem=s_o.at[k],
-            recv_sem=r_o.at[source], device_id={"tp": tp_peer(k)}, device_id_type=MESH,
-        )
-
-    def n_copy(k, source):
-        return pltpu.make_async_remote_copy(
-            src_ref=nall.at[source], dst_ref=nall.at[source], send_sem=s_n.at[k],
-            recv_sem=r_n.at[source], device_id={"tp": tp_peer(k)}, device_id_type=MESH,
-        )
-
-    def m_copy(k, block, source):
-        return pltpu.make_async_remote_copy(
-            src_ref=msend.at[block], dst_ref=mrecv.at[source], send_sem=s_m.at[k],
-            recv_sem=r_m.at[source], device_id={"tp": tp_peer(k)}, device_id_type=MESH,
-        )
-
-    def each(count, step):
-        def body(k, carry):
-            step(k)
-            return carry
-
-        lax.fori_loop(1, count, body, 0)
-
-    row_a = iota((256, 256), 0)
-    row_b = iota((256, 256), 1)
-    perm_s[...] = ones_at(
-        row_b == ((row_a & 63) >> 2) * ROWS + (row_a >> 6) * TOK + (row_a & 3)
-    )
-    permt_s[...] = ones_at(
-        row_a == ((row_b & 63) >> 2) * ROWS + (row_b >> 6) * TOK + (row_b & 3)
-    )
-
-    pl.semaphore_wait(barrier, N_REQ - 1 + N_TP - 1)
-
-    each(N_REQ, lambda k: q8_copy(k, g).start())
     each(N_REQ, lambda k: r8_copy(k, g).start())
 
     load_table.wait()
@@ -238,6 +258,15 @@
             pages_send[c, 2 + s] = page_v[:, c * 128:(c + 1) * 128]
     each(4, lambda k: page_copy(k, x).start())
     pages[x] = pages_send[x]
+
+    row_a = iota((256, 256), 0)
+    row_b = iota((256, 256), 1)
+    perm_s[...] = ones_at(
+        row_b == ((row_a & 63) >> 2) * ROWS + (row_a >> 6) * TOK + (row_a & 3)
+    )
+    permt_s[...] = ones_at(
+        row_a == ((row_b & 63) >> 2) * ROWS + (row_b >> 6) * TOK + (row_b & 3)
+    )
 
     node_m = iota((DRAFT, DRAFT), 0)
     node_n = iota((DRAFT, DRAFT), 1)
@@ -267,14 +296,14 @@
     lo = ones_at(lane_one < HEAD)
     hi = ones_at(lane_one >= HEAD)
 
-    each(N_REQ, lambda k: q8_copy(k, req_peer(k)).wait_recv())
+    await_bytes(q8.at[0:N_REQ - 1], 3)
     load_placement.wait()
     source_group = lax.shift_right_logical(placement[half], 1)
     own_q = q8[source_group]
     qown[...] = own_q
     qall[t] = qown[x]
     each(N_TP, lambda k: q_copy(k, t).start())
-    each(N_REQ, lambda k: r8_copy(k, req_peer(k)).wait_recv())
+    await_bytes(r8.at[0:N_REQ - 1], 5)
     own_kvres = r8[source_group]
     kvall[t_in] = own_kvres[:, 0:256]
     each(HALF, lambda k: kv_copy(k, t_in).start())
@@ -286,8 +315,8 @@
     ones_page = two_ones(span)
     stat_lane = iota((256, 128), 1) & (HEAD - 1)
     load_lengths.wait()
-    each(4, lambda k: page_copy(k, lax.rem(x + k, 4)).wait_recv())
-    each(N_TP, lambda k: q_copy(k, tp_peer(k)).wait_recv())
+    await_bytes(pages.at[0:3], 1)
+    await_bytes(qall.at[0:N_TP - 1], 7)
     for s in range(2):
         valid = row_start * PAGE + iota((1, span), 1) < lengths[s]
         out, lse = softmax_block(
@@ -304,7 +333,7 @@
     each(N_TP, lambda k: o_copy(k, tp_peer(k), t).start())
     orecv[t] = osend[t]
 
-    each(HALF, lambda k: kv_copy(k, lax.rem(t_in + k, HALF)).wait_recv())
+    await_bytes(kvall.at[0:HALF - 1], 9)
     kv_slot = kvall[...].reshape(256, 256)
     accepted = dot(choice, kv_slot)
     for c in range(CHUNKS):
@@ -319,7 +348,7 @@
     ex_row = iota((128, 128), 0)
     expand = ones_at(((ex_row >> 6) == (iota((128, 128), 1) >> 6)) & ((ex_row & (HEAD - 1)) < 3))
 
-    each(N_TP, lambda k: o_copy(k, 0, tp_peer(k)).wait_recv())
+    await_bytes(orecv.at[0:N_TP - 1], 11)
     lse_all = dot(orecv[:, :, 128:256].reshape(N_TP * ROWS, 128), expand)
     lse_all = lse_all.reshape(N_TP // 4, CHUNKS * ROWS, 128)
     out_all = orecv[:, :, 0:128].reshape(N_TP // 4, CHUNKS * ROWS, 128).astype(f32)
@@ -346,17 +375,24 @@
         chunk_s[c * TOK:(c + 1) * TOK, :] = normed[:, c * CW:(c + 1) * CW]
     nall[t] = chunk_s[...].astype(bf16)
 
-    each(N_TP, lambda k: n_copy(k, t).start())
+    for k in FAR:
+        far_copy(k).start()
+    each(N_TP, lambda k: near_start(k))
     expert_row = iota((EXPERTS, GROUP), 0)
     load_ids.wait()
     ids = ids_ref[...]
     picked = expert_row == ids[0:1]
     for k in range(1, ids.shape[0]):
         picked = picked | (expert_row == ids[k:k + 1])
+    for k in FAR:
+        far_copy(k).wait_recv()
+        block = lax.rem(z + 8 - k, 8) * 4 + x
+        for i in range(1, 4):
+            n_copy(block, row_start + lax.rem(x + i, 4)).start()
     load_rw.wait()
     load_gu.wait()
     load_dw.wait()
-    each(N_TP, lambda k: n_copy(k, tp_peer(k)).wait_recv())
+    await_bytes(nall.at[0:N_TP - 1 - len(FAR)], 13)
     for s in range(2):
         rows = dot(perm_s[...], nall[s * HALF:(s + 1) * HALF].reshape(256, CW)).astype(bf16)
         for c in range(CHUNKS):
@@ -389,21 +425,46 @@
             dot(permt_s[...], moe_s[...]).astype(bf16).reshape(HALF, ROWS, CW)
         )
 
-    each(N_TP, lambda k: m_copy(k, tp_peer(k), t).start())
-    mrecv[t] = msend[t]
-    each(4, lambda k: page_copy(k, x).wait_send())
-    each(N_REQ, lambda k: q8_copy(k, g).wait_send())
-    each(N_REQ, lambda k: r8_copy(k, g).wait_send())
-    each(N_TP, lambda k: q_copy(k, t).wait_send())
-    each(HALF, lambda k: kv_copy(k, t_in).wait_send())
-    each(N_TP, lambda k: o_copy(k, 0, t).wait_send())
-    each(N_TP, lambda k: n_copy(k, t).wait_send())
-    each(N_TP, lambda k: m_copy(k, 0, tp_peer(k)).wait_recv())
-    moe_own = jnp.sum(mrecv[...].astype(f32), axis=0)
+    zones = [lax.rem(z + k, 8) for k in (4, 3, 5, 2, 6, 1, 7, 0)]
+    for zone in zones:
+        for k in (1, 3, 2):
+            row_copy(zone, k).start()
+    await_bytes(pages_send.at[0:3], 0)
+    await_bytes(q8.at[0:N_REQ - 1], 2)
+    await_bytes(r8.at[0:N_REQ - 1], 4)
+    await_bytes(qall.at[0:N_TP - 1], 6)
+    await_bytes(kvall.at[0:HALF - 1], 8)
+    await_bytes(osend.at[0:N_TP - 1], 10)
+    await_bytes(nall.at[0:N_TP - 1], 12)
+    for i, zone in enumerate(zones):
+        pltpu.make_async_copy(mrow.at[0:3], mrow.at[0:3], row_sems.at[zone]).wait()
+        part = msend[zone * 4 + x].astype(f32)
+        for k in range(1, 4):
+            part = part + mrow[zone * 4 + lax.rem(x + k, 4)].astype(f32)
+        if i < 7:
+            msum[zone] = part.astype(bf16)
+            zone_copy(zone).start()
+        else:
+            moe_own = part
+    await_bytes(mrecv.at[0:7], 16)
+    for zone in zones[:7]:
+        moe_own = moe_own + mrecv[zone].astype(f32)
     for c in range(CHUNKS):
         flat_s[0:TOK, c * CW:(c + 1) * CW] = moe_own[c * TOK:(c + 1) * TOK, :]
     layer_ref[...] = (hidden + flat_s[0:TOK, :]).astype(bf16)
-    each(N_TP, lambda k: m_copy(k, 0, t).wait_send())
+    await_bytes(msend.at[0:24], 14)
+    await_bytes(msum.at[0:7], 15)
+
+
+def hand_out(attn_in, layer_in, acc_in, attn_out, layer_out, acc_out, sems):
+    copies = [
+        pltpu.make_async_copy(a, b, sems.at[i])
+        for i, (a, b) in enumerate([(attn_in, attn_out), (layer_in, layer_out), (acc_in, acc_out)])
+    ]
+    for copy in copies:
+        copy.start()
+    for copy in copies:
+        copy.wait()
 
 
 def per_device(
@@ -413,13 +474,14 @@
     vmem = pl.BlockSpec(memory_space=pltpu.VMEM)
     hbm = pl.BlockSpec(memory_space=pltpu.MemorySpace.HBM)
     dma = pltpu.SemaphoreType.DMA
-    return pl.pallas_call(
+    shapes = (
+        jax.ShapeDtypeStruct((TOK, D), bf16),
+        jax.ShapeDtypeStruct((TOK, D), bf16),
+        jax.ShapeDtypeStruct((TOK, 1024), bf16),
+    )
+    results = pl.pallas_call(
         kernel,
-        out_shape=(
-            jax.ShapeDtypeStruct((TOK, D), bf16),
-            jax.ShapeDtypeStruct((TOK, D), bf16),
-            jax.ShapeDtypeStruct((TOK, 1024), bf16),
-        ),
+        out_shape=shapes,
         in_specs=[hbm] * 16,
         out_specs=(vmem, vmem, vmem),
         scratch_shapes=[
@@ -451,6 +513,8 @@
             pltpu.VMEM((N_TP, ROWS, CW), bf16),
             pltpu.VMEM((N_TP, ROWS, CW), bf16),
             pltpu.VMEM((N_TP, ROWS, CW), bf16),
+            pltpu.VMEM((8, ROWS, CW), bf16),
+            pltpu.VMEM((8, ROWS, CW), bf16),
             pltpu.VMEM((CHUNKS * ROWS, 128), f32),
             pltpu.VMEM((ROWS, CW), f32),
             pltpu.VMEM((8, D), f32),
@@ -461,10 +525,7 @@
             pltpu.VMEM((GROUP, UNITS_DEV * UNIT), bf16),
             pltpu.VMEM((256, CW), bf16),
             dma((16,)),
-            dma((4,)), dma((4,)),
-            dma((N_REQ,)), dma((N_REQ,)), dma((N_REQ,)), dma((N_REQ,)),
-            dma((N_TP,)), dma((N_TP,)), dma((HALF,)), dma((HALF,)),
-            dma((N_TP,)), dma((N_TP,)), dma((N_TP,)), dma((N_TP,)), dma((N_TP,)), dma((N_TP,)),
+            dma((17,)), dma((8,)), dma((8,)),
         ],
         compiler_params=pltpu.CompilerParams(
             collective_id=0, has_side_effects=True, vmem_limit_bytes=64 << 20
@@ -475,6 +536,15 @@
         cache_keys, cache_values, parents, accept_leaf, out_weight, norm_gain,
         router_weight.T, expert_ids.T, gate_up, down_weight,
     )
+    return pl.pallas_call(
+        hand_out,
+        out_shape=shapes,
+        in_specs=[hbm] * 3,
+        out_specs=(hbm, hbm, hbm),
+        scratch_shapes=[dma((3,))],
+        compiler_params=pltpu.CompilerParams(vmem_limit_bytes=64 << 20),
+        name="hand_out",
+    )(*results)
 
 
 def solution(mesh):

time: 69.8 us -> 58.2 us (0.83)
  Pallas kernels: 64.9 us -> 57.4 us
  local copies, waits for them, and re-layouts: 3.92 us -> 0 us
    pallas_call x1 -> x2, Pallas kernels: 64.9 us -> 57.4 us  [the longest x1 55.3 us: per_device(): pl.pallas_call(kernel, out_shape=shapes, in_specs=[hbm] * 16, out_specs=(...]
    unnamed x3 -> x0, local copies, waits for them, and re-layouts: 3.92 us -> none
where the time goes in v4:
time: 58.2 us; the launch traced here: 58 us
  Pallas kernels  57.4 us (99%)
  between operations  0.65 us (1%)
    pallas_call x1, Pallas kernels, per_device(): pl.pallas_call(kernel, out_shape=shapes, in_specs=[hbm] * 16, out_specs=(...  55.3 us
    pallas_call x1, Pallas kernels, per_device(): pl.pallas_call(hand_out, out_shape=shapes, in_specs=[hbm] * 3, out_specs=...  2.12 us

profile of v4, /device:TPU:2, one launch (start us, length us, event | category | flops | bytes accessed | tf_op | source)
XLA Modules:
  0.0 58.0 jit_solution(11637545173336276972)
XLA Ops:
  0.6 55.3 %verify_layer.1 = (bf16[4,1536]{1,0:T(4,128)(2,1)}, bf16[4,1536]{1,0:T(4,128)(2,1)}, bf16[4,1024]{1,0:T(4,128)(2,1)}) custom-call(bf16[4,1536]{1,0:T(4,128)(2,1)} %q_hbm.1, bf16[4,1024]{1,0:T(4,128)(2,1)} %kv_hbm.1, bf16[4,1536]{1,0:T(4,128)(2,1)} %res_hbm.1, s32[2]{0:T(128)} %placement_hbm.1, s32[2]{0:T(128)} %lengths_hbm.1, s32[2]{0:T(128)} %bitcast.5, ...), custom_call_target="tpu_custom_call" | custom-call | tf_op jit(solution)/shard_map/verify_layer/pallas_call | solution.py:482
  55.9 2.1 %hand_out.1 = (bf16[4,1536]{1,0:T(4,128)(2,1)}, bf16[4,1536]{1,0:T(4,128)(2,1)}, bf16[4,1024]{1,0:T(4,128)(2,1)}) custom-call(bf16[4,1536]{1,0:T(4,128)(2,1)} %get-tuple-element.6.attn_in, bf16[4,1536]{1,0:T(4,128)(2,1)} %get-tuple-element.7.layer_in, bf16[4,1024]{1,0:T(4,128)(2,1)} %get-tuple-element.8.acc_in), custom_call_target="tpu_custom_call" | custom-call | tf_op jit(solution)/shard_map/hand_out/pallas_call | solution.py:539

commit v5 on v4

--- a/solution.py
+++ b/solution.py
@@ -50,10 +50,12 @@
     return lax.dot_general(a, b, (((1,), (1,)), ((), ())), preferred_element_type=f32)
 
 
-def softmax_block(stacked, keys, values, lo, hi, ones_rhs, valid):
-    count = keys.shape[0]
-    keys_two = jnp.concatenate([keys * lo, keys * hi], axis=0)
-    values_two = jnp.concatenate([values * lo, values * hi], axis=0)
+def two_heads(block, lo, hi):
+    return jnp.concatenate([block * lo, block * hi], axis=0)
+
+
+def softmax_block(stacked, keys_two, values_two, valid):
+    count = keys_two.shape[0] // 2
     scores = dot_t(stacked, keys_two)
     s_lo = jnp.where(valid, scores[:, :count], neg_big)
     s_hi = jnp.where(valid, scores[:, count:], neg_big)
@@ -61,11 +63,9 @@
     m_hi = jnp.max(s_hi, axis=1, keepdims=True)
     w_lo = jnp.where(valid, jnp.exp(s_lo - m_lo), 0.0).astype(bf16)
     w_hi = jnp.where(valid, jnp.exp(s_hi - m_hi), 0.0).astype(bf16)
-    weights = jnp.concatenate([w_lo, w_hi], axis=1)
-    both = dot(weights, jnp.concatenate([values_two, ones_rhs], axis=1))
+    both = dot(jnp.concatenate([w_lo, w_hi], axis=1), values_two)
     out, total = both[:, :128], both[:, 128:]
-    rows = out.shape[0]
-    first = iota((rows, 128), 1) < HEAD
+    first = iota((out.shape[0], 128), 1) < HEAD
     top = jnp.where(first, m_lo, m_hi)
     some = total > 0.0
     safe = jnp.where(some, total, 1.0)
@@ -82,10 +82,10 @@
     q_hbm, kv_hbm, res_hbm, placement_hbm, lengths_hbm, table_hbm, keys_hbm, vals_hbm,
     par_hbm, leaf_hbm, ow_hbm, gain_hbm, rw_hbm, ids_hbm, gu_hbm, dw_hbm,
     attn_ref, layer_ref, acc_ref,
-    q_ref, kv_ref, res_ref, placement, lengths, table, kbuf, vbuf,
+    placement, lengths, table, kbuf, vbuf,
     par_ref, leaf, ow, gain_ref, rw, ids_ref, gu, dw,
-    q8, r8, qown, qall, kvall, pages_send, pages, osend, orecv, nall, msend, mrow, msum, mrecv,
-    heads_s, chunk_s, flat_s, res_s, perm_s, permt_s, nfull, act_s, moe_s,
+    q8, kv8, res8, qown, qall, kvall, pages_send, pages, osend, orecv, nall, msend, mrow, msum, mrecv,
+    heads_s, chunk_s, flat_s, perm_s, permt_s, lift_s, kz_s, vz_s, nfull, act_s, moe_s,
     wsem, sems, far_sems, row_sems,
 ):
     g = lax.axis_index("req")
@@ -99,8 +99,14 @@
     def req_peer(k):
         return lax.rem(g + k, N_REQ)
 
+    def offset(k):
+        i, j = (k - 1) // 4, (k - 1) % 4
+        along_z = 4 + (1 - 2 * (i % 2)) * ((i + 1) // 2)
+        return along_z, 2 + (1 - 2 * (j % 2)) * ((j + 1) // 2)
+
     def tp_peer(k):
-        return lax.rem(t // 4 + k // 4, 8) * 4 + lax.rem(t % 4 + k % 4, 4)
+        along_z, along_x = offset(k)
+        return lax.rem(z + along_z, 8) * 4 + lax.rem(x + along_x, 4)
 
     def slot_peer(k):
         return half * HALF + lax.rem(t_in + k, HALF)
@@ -120,11 +126,11 @@
         copy.start()
         return copy
 
-    load_q = load(0, q_hbm, q_ref)
-    load_kv = load(1, kv_hbm, kv_ref)
-    load_res = load(2, res_hbm, res_ref)
     lax.fori_loop(1, N_REQ, greet_req, 0)
     lax.fori_loop(1, N_TP, greet_tp, 0)
+    load_q = load(0, q_hbm, q8.at[g])
+    load_kv = load(1, kv_hbm, kv8.at[g])
+    load_res = load(2, res_hbm, res8.at[g])
     load_placement = load(3, placement_hbm, placement)
     load_par = load(4, par_hbm, par_ref)
     load_leaf = load(5, leaf_hbm, leaf)
@@ -139,16 +145,6 @@
     load_gu = load(14, gu_hbm, gu)
     load_dw = load(15, dw_hbm, dw)
 
-    load_q.wait()
-    q_in = q_ref[...].astype(f32) * (HEAD ** -0.5)
-    heads_s[...] = jnp.zeros_like(heads_s)
-    for c in range(CHUNKS):
-        for r in range(3):
-            for k in range(2):
-                at = c * CW + (k * 3 + r) * HEAD
-                row = c * ROWS + r * TOK
-                heads_s[row:row + TOK, k * HEAD:(k + 1) * HEAD] = q_in[:, at:at + HEAD]
-    q8[g] = heads_s[...].astype(bf16).reshape(CHUNKS, ROWS, 128)
     def page_copy(k, source):
         peer = lax.rem(x + k, 4)
         return pltpu.make_async_remote_copy(
@@ -158,19 +154,25 @@
 
     def q8_copy(k, source):
         return pltpu.make_async_remote_copy(
-            src_ref=q8.at[source], dst_ref=q8.at[source], send_sem=sems.at[2],
+            src_ref=q_hbm, dst_ref=q8.at[source], send_sem=sems.at[2],
             recv_sem=sems.at[3], device_id={"req": req_peer(k)}, device_id_type=MESH,
         )
 
-    def r8_copy(k, source):
-        return pltpu.make_async_remote_copy(
-            src_ref=r8.at[source], dst_ref=r8.at[source], send_sem=sems.at[4],
+    def kv8_copy(k, source):
+        return pltpu.make_async_remote_copy(
+            src_ref=kv_hbm, dst_ref=kv8.at[source], send_sem=sems.at[4],
             recv_sem=sems.at[5], device_id={"req": req_peer(k)}, device_id_type=MESH,
         )
 
+    def res8_copy(k, source):
+        return pltpu.make_async_remote_copy(
+            src_ref=res_hbm, dst_ref=res8.at[source], send_sem=sems.at[17],
+            recv_sem=sems.at[18], device_id={"req": req_peer(k)}, device_id_type=MESH,
+        )
+
     def q_copy(k, source):
         return pltpu.make_async_remote_copy(
-            src_ref=qown.at[lax.rem(x + k % 4, 4)], dst_ref=qall.at[source], send_sem=sems.at[6],
+            src_ref=qown.at[lax.rem(x + offset(k)[1], 4)], dst_ref=qall.at[source], send_sem=sems.at[6],
             recv_sem=sems.at[7], device_id={"tp": tp_peer(k)}, device_id_type=MESH,
         )
 
@@ -213,7 +215,7 @@
         )
 
     def near_start(k):
-        zone = k // 4
+        zone = offset(k)[0]
         far = functools.reduce(jnp.logical_or, [zone == f for f in FAR])
 
         @pl.when(jnp.logical_not(far))
@@ -233,19 +235,8 @@
     pl.semaphore_wait(barrier, N_REQ - 1 + N_TP - 1)
 
     each(N_REQ, lambda k: q8_copy(k, g).start())
-    load_kv.wait()
-    kv_in = kv_ref[...].astype(f32)
-    for c in range(CHUNKS):
-        chunk_s[c * TOK:(c + 1) * TOK, 0:128] = kv_in[:, c * 128:(c + 1) * 128]
-        chunk_s[c * TOK:(c + 1) * TOK, 128:256] = kv_in[:, 512 + c * 128:512 + (c + 1) * 128]
-    r8[g, :, 0:256] = chunk_s[:, 0:256].astype(bf16)
-    load_res.wait()
-    res_in = res_ref[...].astype(f32)
-    for c in range(CHUNKS):
-        chunk_s[c * TOK:(c + 1) * TOK, :] = res_in[:, c * CW:(c + 1) * CW]
-    r8[g, :, 256:640] = chunk_s[...].astype(bf16)
-
-    each(N_REQ, lambda k: r8_copy(k, g).start())
+    each(N_REQ, lambda k: kv8_copy(k, g).start())
+    each(N_REQ, lambda k: res8_copy(k, g).start())
 
     load_table.wait()
     load_keys.wait()
@@ -258,6 +249,37 @@
             pages_send[c, 2 + s] = page_v[:, c * 128:(c + 1) * 128]
     each(4, lambda k: page_copy(k, x).start())
     pages[x] = pages_send[x]
+    lane_one = iota((1, 128), 1)
+    lo = ones_at(lane_one < HEAD)
+    hi = ones_at(lane_one >= HEAD)
+
+    load_q.wait()
+    load_placement.wait()
+    source_group = lax.shift_right_logical(placement[half], 1)
+    heads_s[...] = jnp.zeros_like(heads_s)
+    await_bytes(q8.at[0:N_REQ - 1], 3)
+    q_in = q8[source_group].astype(f32) * (HEAD ** -0.5)
+    for c in range(CHUNKS):
+        for r in range(3):
+            for k in range(2):
+                at = c * CW + (k * 3 + r) * HEAD
+                row = c * ROWS + r * TOK
+                heads_s[row:row + TOK, k * HEAD:(k + 1) * HEAD] = q_in[:, at:at + HEAD]
+    own_q = heads_s[...].astype(bf16).reshape(CHUNKS, ROWS, 128)
+    qown[...] = own_q
+    qall[t] = qown[x]
+    each(N_TP, lambda k: q_copy(k, t).start())
+    load_kv.wait()
+    await_bytes(kv8.at[0:N_REQ - 1], 5)
+    kv_in = kv8[source_group].astype(f32)
+    for c in range(CHUNKS):
+        chunk_s[c * TOK:(c + 1) * TOK, 0:128] = kv_in[:, c * 128:(c + 1) * 128]
+        chunk_s[c * TOK:(c + 1) * TOK, 128:256] = kv_in[:, 512 + c * 128:512 + (c + 1) * 128]
+    kvall[t_in] = chunk_s[:, 0:256].astype(bf16)
+    each(HALF, lambda k: kv_copy(k, t_in).start())
+    load_res.wait()
+    await_bytes(res8.at[0:N_REQ - 1], 18)
+    own_res = res8[source_group].astype(f32)
 
     row_a = iota((256, 256), 0)
     row_b = iota((256, 256), 1)
@@ -267,6 +289,40 @@
     permt_s[...] = ones_at(
         row_a == ((row_b & 63) >> 2) * ROWS + (row_b >> 6) * TOK + (row_b & 3)
     )
+
+    lift_r = iota((256, 768), 0)
+    lift_c = iota((256, 768), 1)
+    lift_s[...] = ones_at(
+        ((lift_r >> 4) == ((lift_c & 255) >> 4)) & ((lift_r & 15) == 3 * TOK + (lift_c >> 8))
+    )
+    span = 4 * PAGE
+    ones_page = two_ones(span)
+    block_row = iota((256, 128), 0) & (ROWS - 1)
+    block_lane = iota((256, 128), 1)
+    diag = (block_lane & (HEAD - 1)) == block_row
+    load_lengths.wait()
+    await_bytes(pages.at[0:3], 1)
+    for s in range(2):
+        kz_s[s] = two_heads(pages[:, s].reshape(span, 128), lo, hi)
+        vz_s[s, :, 0:128] = two_heads(pages[:, 2 + s].reshape(span, 128), lo, hi)
+        vz_s[s, :, 128:256] = ones_page
+    await_bytes(qall.at[0:N_TP - 1], 7)
+    for s in range(2):
+        valid = row_start * PAGE + iota((1, span), 1) < lengths[s]
+        out, lse = softmax_block(
+            qall[s * HALF:(s + 1) * HALF].reshape(256, 128), kz_s[s], vz_s[s], valid
+        )
+        first = lse.astype(bf16).astype(f32)
+        rest = lse - first
+        second = rest.astype(bf16).astype(f32)
+        parts = [jnp.where(diag, part, 0.0).astype(bf16) for part in (first, second, rest - second)]
+        lifted = dot(lift_s[...], jnp.concatenate(parts, axis=0))
+        osend[s * HALF:(s + 1) * HALF] = (
+            jnp.where(block_row < 3 * TOK, out, lifted).astype(bf16).reshape(HALF, ROWS, 128)
+        )
+
+    each(N_TP, lambda k: o_copy(k, tp_peer(k), t).start())
+    orecv[t] = osend[t]
 
     node_m = iota((DRAFT, DRAFT), 0)
     node_n = iota((DRAFT, DRAFT), 1)
@@ -291,48 +347,6 @@
     rank = dot(flags.astype(bf16), ones_at(node_m <= node_n)) - 1.0
     chosen = ones_at((flags > 0.5) & (rank == own_node.astype(f32)))
     choice = jnp.where(same_chunk, dot(chosen, spread), 0.0).astype(bf16)
-
-    lane_one = iota((1, 128), 1)
-    lo = ones_at(lane_one < HEAD)
-    hi = ones_at(lane_one >= HEAD)
-
-    await_bytes(q8.at[0:N_REQ - 1], 3)
-    load_placement.wait()
-    source_group = lax.shift_right_logical(placement[half], 1)
-    own_q = q8[source_group]
-    qown[...] = own_q
-    qall[t] = qown[x]
-    each(N_TP, lambda k: q_copy(k, t).start())
-    await_bytes(r8.at[0:N_REQ - 1], 5)
-    own_kvres = r8[source_group]
-    kvall[t_in] = own_kvres[:, 0:256]
-    each(HALF, lambda k: kv_copy(k, t_in).start())
-    own_res = own_kvres[:, 256:640].astype(f32)
-    for c in range(CHUNKS):
-        res_s[0:TOK, c * CW:(c + 1) * CW] = own_res[c * TOK:(c + 1) * TOK, :]
-
-    span = 4 * PAGE
-    ones_page = two_ones(span)
-    stat_lane = iota((256, 128), 1) & (HEAD - 1)
-    load_lengths.wait()
-    await_bytes(pages.at[0:3], 1)
-    await_bytes(qall.at[0:N_TP - 1], 7)
-    for s in range(2):
-        valid = row_start * PAGE + iota((1, span), 1) < lengths[s]
-        out, lse = softmax_block(
-            qall[s * HALF:(s + 1) * HALF].reshape(256, 128), pages[:, s].reshape(span, 128),
-            pages[:, 2 + s].reshape(span, 128), lo, hi, ones_page, valid,
-        )
-        first = lse.astype(bf16).astype(f32)
-        rest = lse - first
-        second = rest.astype(bf16).astype(f32)
-        stats = jnp.where(stat_lane == 0, first, jnp.where(stat_lane == 1, second, rest - second))
-        osend[s * HALF:(s + 1) * HALF, :, 0:128] = out.astype(bf16).reshape(HALF, ROWS, 128)
-        osend[s * HALF:(s + 1) * HALF, :, 128:256] = stats.astype(bf16).reshape(HALF, ROWS, 128)
-
-    each(N_TP, lambda k: o_copy(k, tp_peer(k), t).start())
-    orecv[t] = osend[t]
-
     await_bytes(kvall.at[0:HALF - 1], 9)
     kv_slot = kvall[...].reshape(256, 256)
     accepted = dot(choice, kv_slot)
@@ -342,16 +356,23 @@
             accepted[c * TOK:(c + 1) * TOK, 128:256].astype(bf16)
         )
     tree_out, tree_lse = softmax_block(
-        own_q.reshape(CHUNKS * ROWS, 128), kv_slot[:, 0:128], kv_slot[:, 128:256], lo, hi,
-        two_ones(256), tree_valid,
-    )
-    ex_row = iota((128, 128), 0)
-    expand = ones_at(((ex_row >> 6) == (iota((128, 128), 1) >> 6)) & ((ex_row & (HEAD - 1)) < 3))
+        own_q.reshape(CHUNKS * ROWS, 128), two_heads(kv_slot[:, 0:128], lo, hi),
+        jnp.concatenate([two_heads(kv_slot[:, 128:256], lo, hi), two_ones(256)], axis=1), tree_valid,
+    )
+    drop = ones_at(
+        ((row_a >> 4) == (row_b >> 4)) & ((row_b & 15) >= 3 * TOK) & ((row_b & 15) < 3 * TOK + 3)
+    )
 
     await_bytes(orecv.at[0:N_TP - 1], 11)
-    lse_all = dot(orecv[:, :, 128:256].reshape(N_TP * ROWS, 128), expand)
-    lse_all = lse_all.reshape(N_TP // 4, CHUNKS * ROWS, 128)
-    out_all = orecv[:, :, 0:128].reshape(N_TP // 4, CHUNKS * ROWS, 128).astype(f32)
+    lse_parts = []
+    for s in range(2):
+        packed = orecv[s * HALF:(s + 1) * HALF].reshape(256, 128)
+        own_lane = jnp.where(diag, dot(drop, packed), 0.0)
+        lse_lo = jnp.sum(jnp.where(block_lane < HEAD, own_lane, 0.0), axis=1, keepdims=True)
+        lse_hi = jnp.sum(jnp.where(block_lane < HEAD, 0.0, own_lane), axis=1, keepdims=True)
+        lse_parts.append(jnp.where(block_lane < HEAD, lse_lo, lse_hi))
+    lse_all = jnp.concatenate(lse_parts, axis=0).reshape(N_TP // 4, CHUNKS * ROWS, 128)
+    out_all = orecv[...].reshape(N_TP // 4, CHUNKS * ROWS, 128).astype(f32)
     top = jnp.maximum(jnp.max(lse_all, axis=0), tree_lse)
     scale = jnp.exp(lse_all - top[None])
     tree_scale = jnp.exp(tree_lse - top)
@@ -368,7 +389,7 @@
 
     load_ow.wait()
     load_gain.wait()
-    hidden = res_s[0:TOK, :] + dot(attn, ow[...])
+    hidden = own_res + dot(attn, ow[...])
     mean = jnp.mean(hidden * hidden, axis=-1, keepdims=True)
     normed = (hidden * lax.rsqrt(mean + norm_eps) * gain_ref[...]).astype(bf16).astype(f32)
     for c in range(CHUNKS):
@@ -427,11 +448,12 @@
 
     zones = [lax.rem(z + k, 8) for k in (4, 3, 5, 2, 6, 1, 7, 0)]
     for zone in zones:
-        for k in (1, 3, 2):
+        for k in (2, 1, 3):
             row_copy(zone, k).start()
     await_bytes(pages_send.at[0:3], 0)
     await_bytes(q8.at[0:N_REQ - 1], 2)
-    await_bytes(r8.at[0:N_REQ - 1], 4)
+    await_bytes(kv8.at[0:N_REQ - 1], 4)
+    await_bytes(res8.at[0:N_REQ - 1], 17)
     await_bytes(qall.at[0:N_TP - 1], 6)
     await_bytes(kvall.at[0:HALF - 1], 8)
     await_bytes(osend.at[0:N_TP - 1], 10)
@@ -456,15 +478,10 @@
     await_bytes(msum.at[0:7], 15)
 
 
-def hand_out(attn_in, layer_in, acc_in, attn_out, layer_out, acc_out, sems):
-    copies = [
-        pltpu.make_async_copy(a, b, sems.at[i])
-        for i, (a, b) in enumerate([(attn_in, attn_out), (layer_in, layer_out), (acc_in, acc_out)])
-    ]
-    for copy in copies:
-        copy.start()
-    for copy in copies:
-        copy.wait()
+def hand_out(attn_in, layer_in, acc_in, attn_out, layer_out, acc_out):
+    attn_out[...] = attn_in[...]
+    layer_out[...] = layer_in[...]
+    acc_out[...] = acc_in[...]
 
 
 def per_device(
@@ -485,9 +502,6 @@
         in_specs=[hbm] * 16,
         out_specs=(vmem, vmem, vmem),
         scratch_shapes=[
-            pltpu.VMEM((TOK, D), bf16),
-            pltpu.VMEM((TOK, 1024), bf16),
-            pltpu.VMEM((TOK, D), bf16),
             pltpu.SMEM((2,), jnp.int32),
             pltpu.SMEM((2,), jnp.int32),
             pltpu.SMEM((2,), jnp.int32),
@@ -501,15 +515,16 @@
             pltpu.VMEM((8, GROUP), jnp.int32),
             pltpu.VMEM((UNITS_DEV, D, 2 * UNIT), bf16),
             pltpu.VMEM((UNITS_DEV, UNIT, D), bf16),
-            pltpu.VMEM((N_REQ, CHUNKS, ROWS, 128), bf16),
-            pltpu.VMEM((N_REQ, ROWS, 640), bf16),
+            pltpu.VMEM((N_REQ, TOK, D), bf16),
+            pltpu.VMEM((N_REQ, TOK, 1024), bf16),
+            pltpu.VMEM((N_REQ, TOK, D), bf16),
             pltpu.VMEM((CHUNKS, ROWS, 128), bf16),
             pltpu.VMEM((N_TP, ROWS, 128), bf16),
             pltpu.VMEM((HALF, ROWS, 256), bf16),
             pltpu.VMEM((CHUNKS, 4, PAGE, 128), bf16),
             pltpu.VMEM((4, 4, PAGE, 128), bf16),
-            pltpu.VMEM((N_TP, ROWS, 256), bf16),
-            pltpu.VMEM((N_TP, ROWS, 256), bf16),
+            pltpu.VMEM((N_TP, ROWS, 128), bf16),
+            pltpu.VMEM((N_TP, ROWS, 128), bf16),
             pltpu.VMEM((N_TP, ROWS, CW), bf16),
             pltpu.VMEM((N_TP, ROWS, CW), bf16),
             pltpu.VMEM((N_TP, ROWS, CW), bf16),
@@ -518,14 +533,16 @@
             pltpu.VMEM((CHUNKS * ROWS, 128), f32),
             pltpu.VMEM((ROWS, CW), f32),
             pltpu.VMEM((8, D), f32),
-            pltpu.VMEM((8, D), f32),
             pltpu.VMEM((256, 256), bf16),
             pltpu.VMEM((256, 256), bf16),
+            pltpu.VMEM((256, 768), bf16),
+            pltpu.VMEM((2, 8 * PAGE, 128), bf16),
+            pltpu.VMEM((2, 8 * PAGE, 256), bf16),
             pltpu.VMEM((GROUP, D), bf16),
             pltpu.VMEM((GROUP, UNITS_DEV * UNIT), bf16),
             pltpu.VMEM((256, CW), bf16),
             dma((16,)),
-            dma((17,)), dma((8,)), dma((8,)),
+            dma((19,)), dma((8,)), dma((8,)),
         ],
         compiler_params=pltpu.CompilerParams(
             collective_id=0, has_side_effects=True, vmem_limit_bytes=64 << 20
@@ -539,9 +556,8 @@
     return pl.pallas_call(
         hand_out,
         out_shape=shapes,
-        in_specs=[hbm] * 3,
-        out_specs=(hbm, hbm, hbm),
-        scratch_shapes=[dma((3,))],
+        in_specs=[vmem] * 3,
+        out_specs=(vmem, vmem, vmem),
         compiler_params=pltpu.CompilerParams(vmem_limit_bytes=64 << 20),
         name="hand_out",
     )(*results)

time: 58.2 us -> 52.8 us (0.907)
  Pallas kernels: 57.4 us -> 51.8 us
    pallas_call x1, Pallas kernels: 55.3 us -> 50.4 us  [per_device(): pl.pallas_call(kernel, out_shape=shapes, in_specs=[hbm] * 16, out_specs=(...]
    pallas_call x1, Pallas kernels: 2.12 us -> 1.34 us  [per_device(): pl.pallas_call(hand_out, out_shape=shapes, in_specs=[vmem] * 3, out_specs...]
where the time goes in v5:
time: 52.8 us; the launch traced here: 52.4 us
  Pallas kernels  51.8 us (98%)
  between operations  0.65 us (1%)
    pallas_call x1, Pallas kernels, per_device(): pl.pallas_call(kernel, out_shape=shapes, in_specs=[hbm] * 16, out_specs=(...  50.4 us
    pallas_call x1, Pallas kernels, per_device(): pl.pallas_call(hand_out, out_shape=shapes, in_specs=[vmem] * 3, out_specs...  1.34 us

profile of v5, /device:TPU:2, one launch (start us, length us, event | category | flops | bytes accessed | tf_op | source)
XLA Modules:
  0.0 52.4 jit_solution(1213086222333186485)
XLA Ops:
  0.6 50.4 %verify_layer.1 = (bf16[4,1536]{1,0:T(4,128)(2,1)}, bf16[4,1536]{1,0:T(4,128)(2,1)}, bf16[4,1024]{1,0:T(4,128)(2,1)}) custom-call(bf16[4,1536]{1,0:T(4,128)(2,1)} %q_hbm.1, bf16[4,1024]{1,0:T(4,128)(2,1)} %kv_hbm.1, bf16[4,1536]{1,0:T(4,128)(2,1)} %res_hbm.1, s32[2]{0:T(128)} %placement_hbm.1, s32[2]{0:T(128)} %lengths_hbm.1, s32[2]{0:T(128)} %bitcast.5, ...), custom_call_target="tpu_custom_call" | custom-call | tf_op jit(solution)/shard_map/verify_layer/pallas_call | solution.py:499
  51.1 1.3 %hand_out.1 = (bf16[4,1536]{1,0:T(4,128)(2,1)}, bf16[4,1536]{1,0:T(4,128)(2,1)}, bf16[4,1024]{1,0:T(4,128)(2,1)}) custom-call(bf16[4,1536]{1,0:T(4,128)(2,1)} %get-tuple-element.6.attn_in, bf16[4,1536]{1,0:T(4,128)(2,1)} %get-tuple-element.7.layer_in, bf16[4,1024]{1,0:T(4,128)(2,1)} %get-tuple-element.8.acc_in), custom_call_target="tpu_custom_call" | custom-call | tf_op jit(solution)/shard_map/hand_out/pallas_call | solution.py:556

commit v6 on v5

--- a/solution.py
+++ b/solution.py
@@ -25,7 +25,7 @@
 HALF = N_TP // 2
 ROWS = CHUNKS * TOK
 GROUP = N_TP * TOK
-FAR = (3, 5, 4)
+FAR = (2, 6, 3, 5, 4)
 
 neg_big = -1e30
 norm_eps = 1e-06
@@ -84,7 +84,7 @@
     attn_ref, layer_ref, acc_ref,
     placement, lengths, table, kbuf, vbuf,
     par_ref, leaf, ow, gain_ref, rw, ids_ref, gu, dw,
-    q8, kv8, res8, qown, qall, kvall, pages_send, pages, osend, orecv, nall, msend, mrow, msum, mrecv,
+    q8, kv8, res8, qown, qall, kvall, pages_send, pages, osend, orecv, nall, msend, mrow, msum, mnear, mrecv,
     heads_s, chunk_s, flat_s, perm_s, permt_s, lift_s, kz_s, vz_s, nfull, act_s, moe_s,
     wsem, sems, far_sems, row_sems,
 ):
@@ -173,7 +173,7 @@
     def q_copy(k, source):
         return pltpu.make_async_remote_copy(
             src_ref=qown.at[lax.rem(x + offset(k)[1], 4)], dst_ref=qall.at[source], send_sem=sems.at[6],
-            recv_sem=sems.at[7], device_id={"tp": tp_peer(k)}, device_id_type=MESH,
+            recv_sem=sems.at[19], device_id={"tp": tp_peer(k)}, device_id_type=MESH,
         )
 
     def kv_copy(k, source):
@@ -221,6 +221,13 @@
         @pl.when(jnp.logical_not(far))
         def _():
             n_copy(t, tp_peer(k)).start()
+
+    def direct_copy(along_z, k):
+        peer = lax.rem(z + along_z, 8) * 4 + lax.rem(x + k, 4)
+        return pltpu.make_async_remote_copy(
+            src_ref=msend.at[peer], dst_ref=mnear.at[t], send_sem=sems.at[14],
+            recv_sem=sems.at[7], device_id={"tp": peer}, device_id_type=MESH,
+        )
 
     def await_bytes(refs, index):
         pltpu.make_async_copy(refs, refs, sems.at[index]).wait()
@@ -306,7 +313,7 @@
         kz_s[s] = two_heads(pages[:, s].reshape(span, 128), lo, hi)
         vz_s[s, :, 0:128] = two_heads(pages[:, 2 + s].reshape(span, 128), lo, hi)
         vz_s[s, :, 128:256] = ones_page
-    await_bytes(qall.at[0:N_TP - 1], 7)
+    await_bytes(qall.at[0:N_TP - 1], 19)
     for s in range(2):
         valid = row_start * PAGE + iota((1, span), 1) < lengths[s]
         out, lse = softmax_block(
@@ -446,10 +453,15 @@
             dot(permt_s[...], moe_s[...]).astype(bf16).reshape(HALF, ROWS, CW)
         )
 
-    zones = [lax.rem(z + k, 8) for k in (4, 3, 5, 2, 6, 1, 7, 0)]
+    zones = [lax.rem(z + k, 8) for k in (4, 3, 5)]
     for zone in zones:
         for k in (2, 1, 3):
             row_copy(zone, k).start()
+    for along_z in (2, 6, 1, 7):
+        for k in (2, 1, 3, 0):
+            direct_copy(along_z, k).start()
+    for k in (2, 1, 3):
+        direct_copy(0, k).start()
     await_bytes(pages_send.at[0:3], 0)
     await_bytes(q8.at[0:N_REQ - 1], 2)
     await_bytes(kv8.at[0:N_REQ - 1], 4)
@@ -463,19 +475,23 @@
         part = msend[zone * 4 + x].astype(f32)
         for k in range(1, 4):
             part = part + mrow[zone * 4 + lax.rem(x + k, 4)].astype(f32)
-        if i < 7:
-            msum[zone] = part.astype(bf16)
-            zone_copy(zone).start()
-        else:
-            moe_own = part
-    await_bytes(mrecv.at[0:7], 16)
-    for zone in zones[:7]:
+        msum[zone] = part.astype(bf16)
+        zone_copy(zone).start()
+    moe_own = msend[t].astype(f32)
+    await_bytes(mnear.at[0:19], 7)
+    for along_z in (2, 6, 1, 7):
+        for k in range(4):
+            moe_own = moe_own + mnear[lax.rem(z + along_z, 8) * 4 + lax.rem(x + k, 4)].astype(f32)
+    for k in range(1, 4):
+        moe_own = moe_own + mnear[z * 4 + lax.rem(x + k, 4)].astype(f32)
+    await_bytes(mrecv.at[0:3], 16)
+    for zone in zones:
         moe_own = moe_own + mrecv[zone].astype(f32)
     for c in range(CHUNKS):
         flat_s[0:TOK, c * CW:(c + 1) * CW] = moe_own[c * TOK:(c + 1) * TOK, :]
     layer_ref[...] = (hidden + flat_s[0:TOK, :]).astype(bf16)
-    await_bytes(msend.at[0:24], 14)
-    await_bytes(msum.at[0:7], 15)
+    await_bytes(msend.at[0:28], 14)
+    await_bytes(msum.at[0:3], 15)
 
 
 def hand_out(attn_in, layer_in, acc_in, attn_out, layer_out, acc_out):
@@ -498,7 +514,7 @@
     )
     results = pl.pallas_call(
         kernel,
-        out_shape=shapes,
+        out_shape=tuple(pltpu.VMEM(a.shape, a.dtype) for a in shapes),
         in_specs=[hbm] * 16,
         out_specs=(vmem, vmem, vmem),
         scratch_shapes=[
@@ -529,6 +545,7 @@
             pltpu.VMEM((N_TP, ROWS, CW), bf16),
             pltpu.VMEM((N_TP, ROWS, CW), bf16),
             pltpu.VMEM((8, ROWS, CW), bf16),
+            pltpu.VMEM((N_TP, ROWS, CW), bf16),
             pltpu.VMEM((8, ROWS, CW), bf16),
             pltpu.VMEM((CHUNKS * ROWS, 128), f32),
             pltpu.VMEM((ROWS, CW), f32),
@@ -542,10 +559,10 @@
             pltpu.VMEM((GROUP, UNITS_DEV * UNIT), bf16),
             pltpu.VMEM((256, CW), bf16),
             dma((16,)),
-            dma((19,)), dma((8,)), dma((8,)),
+            dma((20,)), dma((8,)), dma((8,)),
         ],
         compiler_params=pltpu.CompilerParams(
-            collective_id=0, has_side_effects=True, vmem_limit_bytes=64 << 20
+            collective_id=0, has_side_effects=True, vmem_limit_bytes=63 << 20
         ),
         name="verify_layer",
     )(
@@ -558,9 +575,9 @@
         out_shape=shapes,
         in_specs=[vmem] * 3,
         out_specs=(vmem, vmem, vmem),
-        compiler_params=pltpu.CompilerParams(vmem_limit_bytes=64 << 20),
+        compiler_params=pltpu.CompilerParams(vmem_limit_bytes=63 << 20),
         name="hand_out",
-    )(*results)
+    )(*(pltpu.with_memory_space_constraint(a, pltpu.VMEM) for a in results))
 
 
 def solution(mesh):

time: 52.8 us -> 51 us (0.966)
  Pallas kernels: 51.8 us -> 50.1 us
    pallas_call x1, Pallas kernels: 50.4 us -> 49.5 us  [per_device(): pl.pallas_call(kernel, out_shape=tuple((pltpu.VMEM(a.shape, a.dtype) for...]
    pallas_call x1, Pallas kernels: 1.34 us -> 0.61 us  [per_device(): pl.pallas_call(hand_out, out_shape=shapes, in_specs=[vmem] * 3, out_specs...]
where the time goes in v6:
time: 51 us; the launch traced here: 50.7 us
  Pallas kernels  50.1 us (98%)
  between operations  0.65 us (1%)
    pallas_call x1, Pallas kernels, per_device(): pl.pallas_call(kernel, out_shape=tuple((pltpu.VMEM(a.shape, a.dtype) for...  49.5 us

profile of v6, /device:TPU:2, one launch (start us, length us, event | category | flops | bytes accessed | tf_op | source)
XLA Modules:
  0.0 50.7 jit_solution(12968085494842008880)
XLA Ops:
  0.6 49.5 %verify_layer.1 = (bf16[4,1536]{1,0:T(4,128)(2,1)S(1)}, bf16[4,1536]{1,0:T(4,128)(2,1)S(1)}, bf16[4,1024]{1,0:T(4,128)(2,1)S(1)}) custom-call(bf16[4,1536]{1,0:T(4,128)(2,1)} %q_hbm.1, bf16[4,1024]{1,0:T(4,128)(2,1)} %kv_hbm.1, bf16[4,1536]{1,0:T(4,128)(2,1)} %res_hbm.1, s32[2]{0:T(128)} %placement_hbm.1, s32[2]{0:T(128)} %lengths_hbm.1, s32[2]{0:T(128)} %bitcast.5, ...), custom_call_target="tpu_custom_call" | custom-call | tf_op jit(solution)/shard_map/verify_layer/pallas_call | solution.py:515
  50.1 0.6 %hand_out.1 = (bf16[4,1536]{1,0:T(4,128)(2,1)}, bf16[4,1536]{1,0:T(4,128)(2,1)}, bf16[4,1024]{1,0:T(4,128)(2,1)}) custom-call(bf16[4,1536]{1,0:T(4,128)(2,1)S(1)} %get-tuple-element.6.attn_in, bf16[4,1536]{1,0:T(4,128)(2,1)S(1)} %get-tuple-element.7.layer_in, bf16[4,1024]{1,0:T(4,128)(2,1)S(1)} %get-tuple-element.8.acc_in), custom_call_target="tpu_custom_call" | custom-call | tf_op jit(solution)/shard_map/hand_out/pallas_call | solution.py:573

commit v7 on v6

--- a/solution.py
+++ b/solution.py
@@ -61,15 +61,14 @@
     s_hi = jnp.where(valid, scores[:, count:], neg_big)
     m_lo = jnp.max(s_lo, axis=1, keepdims=True)
     m_hi = jnp.max(s_hi, axis=1, keepdims=True)
-    w_lo = jnp.where(valid, jnp.exp(s_lo - m_lo), 0.0).astype(bf16)
-    w_hi = jnp.where(valid, jnp.exp(s_hi - m_hi), 0.0).astype(bf16)
+    w_lo = jnp.exp(s_lo - m_lo).astype(bf16)
+    w_hi = jnp.exp(s_hi - m_hi).astype(bf16)
     both = dot(jnp.concatenate([w_lo, w_hi], axis=1), values_two)
     out, total = both[:, :128], both[:, 128:]
     first = iota((out.shape[0], 128), 1) < HEAD
     top = jnp.where(first, m_lo, m_hi)
-    some = total > 0.0
-    safe = jnp.where(some, total, 1.0)
-    return out / safe, jnp.where(some, top + jnp.log(safe), neg_big)
+    some = top > 0.5 * neg_big
+    return out / total, jnp.where(some, top + jnp.log(total), neg_big)
 
 
 def two_ones(count):
@@ -97,7 +96,7 @@
     t_in = t % HALF
 
     def req_peer(k):
-        return lax.rem(g + k, N_REQ)
+        return lax.rem(g + 4 + (1 - 2 * ((k - 1) % 2)) * (k // 2), N_REQ)
 
     def offset(k):
         i, j = (k - 1) // 4, (k - 1) % 4

time: 51 us -> 50.9 us (level)
  no operation moved by 1% of the time
where the time goes in v7:
time: 50.9 us; the launch traced here: 50.7 us
  Pallas kernels  50 us (98%)
  between operations  0.65 us (1%)
    pallas_call x1, Pallas kernels, per_device(): pl.pallas_call(kernel, out_shape=tuple((pltpu.VMEM(a.shape, a.dtype) for...  49.4 us

profile of v7, /device:TPU:2, one launch (start us, length us, event | category | flops | bytes accessed | tf_op | source)
XLA Modules:
  0.0 50.7 jit_solution(4477855580084837290)
XLA Ops:
  0.6 49.4 %verify_layer.1 = (bf16[4,1536]{1,0:T(4,128)(2,1)S(1)}, bf16[4,1536]{1,0:T(4,128)(2,1)S(1)}, bf16[4,1024]{1,0:T(4,128)(2,1)S(1)}) custom-call(bf16[4,1536]{1,0:T(4,128)(2,1)} %q_hbm.1, bf16[4,1024]{1,0:T(4,128)(2,1)} %kv_hbm.1, bf16[4,1536]{1,0:T(4,128)(2,1)} %res_hbm.1, s32[2]{0:T(128)} %placement_hbm.1, s32[2]{0:T(128)} %lengths_hbm.1, s32[2]{0:T(128)} %bitcast.5, ...), custom_call_target="tpu_custom_call" | custom-call | tf_op jit(solution)/shard_map/verify_layer/pallas_call | solution.py:514
  50.1 0.6 %hand_out.1 = (bf16[4,1536]{1,0:T(4,128)(2,1)}, bf16[4,1536]{1,0:T(4,128)(2,1)}, bf16[4,1024]{1,0:T(4,128)(2,1)}) custom-call(bf16[4,1536]{1,0:T(4,128)(2,1)S(1)} %get-tuple-element.6.attn_in, bf16[4,1536]{1,0:T(4,128)(2,1)S(1)} %get-tuple-element.7.layer_in, bf16[4,1024]{1,0:T(4,128)(2,1)S(1)} %get-tuple-element.8.acc_in), custom_call_target="tpu_custom_call" | custom-call | tf_op jit(solution)/shard_map/hand_out/pallas_call | solution.py:572
